TPU v7x, 256 devices: a whole 4x4x8 slice. The times are simulated.
256 devices in a mesh: shard: 8 (over y, core), tensor: 4 (over x), section: 8 (over z).
Axes of the slice: x: 4, y: 4, z: 8, core: 2. Of those that a mesh axis runs over, the one named last changes fastest.
Arguments:
- normed_inputs: bfloat16 [65536, 4096], P(('shard', 'section')), may hold values from -320 to 320
- projection_cotangent: bfloat16 [65536, 2, 1024], P(('shard', 'section'), None, 'tensor'), may hold values from -1 to 1
- small_partials: bfloat16 [64, 10, 4096], P(('shard', 'section'), None, 'tensor'), may hold values from -2000 to 2000
- master_weights: float32 [4096, 2, 1024], P(('shard', 'section'), None, 'tensor'), may hold values from -4 to 4
- first_moment: float32 [4096, 2, 1024], P(('shard', 'section'), None, 'tensor'), may hold values from -3 to 3
- second_moment: float32 [4096, 2, 1024], P(('shard', 'section'), None, 'tensor'), may hold values from 0.05 to 1
- small_master: float32 [10, 4096], P(None, 'tensor'), may hold values from -4 to 4
- small_first: float32 [10, 4096], P(None, 'tensor'), may hold values from -3 to 3
- small_second: float32 [10, 4096], P(None, 'tensor'), may hold values from 0.05 to 1
Outputs:
- updated_master: float32 [4096, 2, 1024], P(('shard', 'section'), None, 'tensor')
- updated_first: float32 [4096, 2, 1024], P(('shard', 'section'), None, 'tensor')
- updated_second: float32 [4096, 2, 1024], P(('shard', 'section'), None, 'tensor')
- gathered_weights: bfloat16 [4096, 2, 1024], P(None, None, 'tensor')
- small_updated_master: float32 [10, 4096], P(None, 'tensor')
- small_updated_first: float32 [10, 4096], P(None, 'tensor')
- small_updated_second: float32 [10, 4096], P(None, 'tensor')
- small_weights: bfloat16 [10, 4096], P(None, 'tensor')
All inputs are finite; a program needn't handle non-finite values.
Results may differ from a plain program's by a relative error of at most 0.0015.
Values may be sent and summed in bfloat16 or wider, within the bound.
A program may use at most 64 MiB of HBM per device.

v0:
```python
import math

import jax
import jax.numpy as jnp
from jax import lax
from jax.sharding import PartitionSpec as P

D = 4096
EXPERTS = 8
STEP = 10
KV_COLS = 1024
SMALL_ROWS = 10


beta_one = 0.9
beta_two = 0.95
learning_rate = 0.01
weight_decay = 0.1
epsilon = 1e-08
clip_factor = 0.5


def adamw(gradient, scale, first, second, master, decay):
    clipped = gradient * scale
    first_new = beta_one * first + (1.0 - beta_one) * clipped
    second_new = beta_two * second + (1.0 - beta_two) * clipped * clipped
    first_hat = first_new / (1.0 - beta_one**STEP)
    second_hat = second_new / (1.0 - beta_two**STEP)
    master_new = master - learning_rate * (
        first_hat / (jnp.sqrt(second_hat) + epsilon) + decay * master
    )
    return (master_new, first_new, second_new)


def body(
    normed_inputs,
    projection_cotangent,
    small_partials,
    master_weights,
    first_moment,
    second_moment,
    small_master,
    small_first,
    small_second,
):
    gradient = lax.psum_scatter(
        jnp.einsum(
            "tf,tjc->fjc", normed_inputs, projection_cotangent, preferred_element_type=jnp.float32
        ),
        ("shard", "section"),
        scatter_dimension=0,
        tiled=True,
    )
    owned_squares = jnp.sum(gradient * gradient)
    local_small = small_partials[0].astype(jnp.float32)
    small_gradient = lax.psum(local_small, ("shard", "section"))
    big_total = lax.psum(owned_squares, ("shard", "tensor", "section"))
    small_total = lax.psum(jnp.sum(small_gradient * small_gradient), "tensor")
    total = big_total + small_total
    limit = clip_factor * math.sqrt(2 * D * KV_COLS + SMALL_ROWS * D)
    scale = jnp.minimum(1.0, limit / (jnp.sqrt(total) + 1e-06))
    master_new, first_new, second_new = adamw(
        gradient, scale, first_moment, second_moment, master_weights, weight_decay
    )
    row_decay = jnp.where(jnp.arange(SMALL_ROWS)[:, None] < EXPERTS, weight_decay, 0.0).astype(
        jnp.float32
    )
    small_master_new, small_first_new, small_second_new = adamw(
        small_gradient, scale, small_first, small_second, small_master, row_decay
    )
    owned_weights = master_new.astype(jnp.bfloat16)
    gathered = lax.all_gather(owned_weights, ("shard", "section"), axis=0, tiled=True)
    return (
        master_new,
        first_new,
        second_new,
        gathered,
        small_master_new,
        small_first_new,
        small_second_new,
        small_master_new.astype(jnp.bfloat16),
    )


def solution(mesh):
    placed = (
        P(("shard", "section"), None),
        P(("shard", "section"), None, "tensor"),
        P(("shard", "section"), None, "tensor"),
        P(("shard", "section"), None, "tensor"),
        P(("shard", "section"), None, "tensor"),
        P(("shard", "section"), None, "tensor"),
        P(None, "tensor"),
        P(None, "tensor"),
        P(None, "tensor"),
    )
    return jax.shard_map(
        body,
        mesh=mesh,
        in_specs=placed,
        out_specs=(
            P(("shard", "section"), None, "tensor"),
            P(("shard", "section"), None, "tensor"),
            P(("shard", "section"), None, "tensor"),
            P(None, None, "tensor"),
            P(None, "tensor"),
            P(None, "tensor"),
            P(None, "tensor"),
            P(None, "tensor"),
        ),
        check_vma=False,
    )
```

profile of v0, /device:TPU:1, one launch (start us, length us, event | category | flops | bytes accessed | tf_op | source)
XLA Modules:
  0.0 454.1 jit_solution(6464595801956574734)
XLA Ops:
  7.2 0.0 copy-start
  7.2 0.0 reduce-scatter.2.cloned.1.call-start
  7.2 1.2 copy-done
  8.4 10.3 %fusion = f32[4096,2,256]{2,0,1:T(8,128)} fusion(bf16[1024,4096]{1,0:T(8,128)(2,1)} %param.9, bf16[1024,2,256]{2,1,0:T(2,128)(2,1)S(1)} %copy-done), kind=kOutput, calls=%fused_computation | convolution fusion | flops 4294967296 | bytes 17825792 | tf_op jit(solution)/shard_map/tf,tjc->fjc/dot_general | solution.py:47
  18.8 0.0 copy-start.4
  18.8 0.0 copy-start.5
  18.8 0.0 copy-start.6
  18.8 0.0 reduce-scatter.2.cloned.1.call-update
  18.8 0.0 all-gather.2.cloned.1.call-start
  18.9 0.6 copy-done.7
  19.5 246.8 %psum.22 = f32[10,1024]{1,0:T(8,128)S(1)} all-reduce(f32[10,1024]{1,0:T(8,128)S(1)} %bitcast_convert_fusion), channel_id=1, replica_groups=mesh['shard'=8,'tensor'=4,'section'=8] {'shard','section'}, use_global_device_ids=true, to_apply=%region_3.0 | all-reduce | flops 10240 | bytes 81920 | tf_op jit(solution)/shard_map/psum | solution.py:56
  266.3 0.6 multiply_reduce_fusion.1
  266.9 1.5 multiply_reduce_fusion
  268.4 9.4 %psum.23 = f32[]{:T(128)} all-reduce(f32[]{:T(128)} %multiply_reduce_fusion.1), channel_id=1, replica_groups=mesh['shard'=8,'tensor'=4,'section'=8] {'tensor'}, use_global_device_ids=true, to_apply=%region_5.0 | all-reduce | flops 1 | bytes 8 | tf_op jit(solution)/shard_map/psum | solution.py:58
  277.9 81.1 %psum.21 = f32[]{:T(128)} all-reduce(f32[]{:T(128)} %multiply_reduce_fusion), channel_id=1, replica_groups=mesh['shard'=8,'tensor'=4,'section'=8] {'shard','tensor','section'}, use_global_device_ids=true, to_apply=%region_2.0 | all-reduce | flops 1 | bytes 8 | tf_op jit(solution)/shard_map/psum | solution.py:57
  360.4 1.7 fusion.8
  362.1 0.0 all-gather.2.cloned.1.call-update
  362.1 0.8 copy.23
  362.9 0.8 copy.24
  363.6 0.8 copy.25
  364.4 0.0 copy-done.5
  364.4 0.7 fusion.6
  365.1 72.0 %all-gather.2.cloned.1.call-done = bf16[4096,2,256]{2,0,1:T(8,128)(2,1)} async-done(((bf16[64,2,256]{2,0,1:T(8,128)(2,1)}), bf16[4096,2,256]{2,0,1:T(8,128)(2,1)}) %all-gather.2.cloned.1.call-update) | async-done | bytes 4194320 | tf_op jit(solution)/shard_map/all_gather | solution.py:72
  437.1 10.1 %copy.26 = bf16[4096,2,256]{2,1,0:T(2,128)(2,1)} copy(bf16[4096,2,256]{2,0,1:T(8,128)(2,1)} %all-gather.2.cloned.1.call-done) | data formatting | bytes 8388608
  (12 shorter events, 0.0 us)
Async XLA Ops:
  7.2 1.2 copy-start
  7.2 259.7 %reduce-scatter.2.cloned.1.call-start = ((), (), s32[]{:S(2)}) async-start(), calls=%async_computation.1 | async-start | bytes 8519680 | tf_op jit(solution)/shard_map/reduce_scatter | solution.py:46
  18.7 0.8 copy-start.7
  18.7 341.7 %copy-start.1 = (f32[64,2,256]{2,1,0:T(2,128)S(1)}, f32[64,2,256]{2,1,0:T(2,128)}, u32[]{:S(2)}) copy-start(f32[64,2,256]{2,1,0:T(2,128)} %param.12) | copy-start | bytes 393220
  18.7 341.7 %copy-start.2 = (f32[64,2,256]{2,1,0:T(2,128)S(1)}, f32[64,2,256]{2,1,0:T(2,128)}, u32[]{:S(2)}) copy-start(f32[64,2,256]{2,1,0:T(2,128)} %param.13) | copy-start | bytes 393220
  18.8 341.7 %copy-start.3 = (f32[64,2,256]{2,1,0:T(2,128)S(1)}, f32[64,2,256]{2,1,0:T(2,128)}, u32[]{:S(2)}) copy-start(f32[64,2,256]{2,1,0:T(2,128)} %param.14) | copy-start | bytes 393220
  18.8 345.6 %copy-start.4 = (f32[10,1024]{1,0:T(8,128)S(1)}, f32[10,1024]{1,0:T(8,128)}, u32[]{:S(2)}) copy-start(f32[10,1024]{1,0:T(8,128)} %param.15) | copy-start | bytes 122884
  18.8 345.6 %copy-start.5 = (f32[10,1024]{1,0:T(8,128)S(1)}, f32[10,1024]{1,0:T(8,128)}, u32[]{:S(2)}) copy-start(f32[10,1024]{1,0:T(8,128)} %param.16) | copy-start | bytes 122884
  18.8 345.6 %copy-start.6 = (f32[10,1024]{1,0:T(8,128)S(1)}, f32[10,1024]{1,0:T(8,128)}, u32[]{:S(2)}) copy-start(f32[10,1024]{1,0:T(8,128)} %param.17) | copy-start | bytes 122884
  18.8 418.3 %all-gather.2.cloned.1.call-start = ((), (), s32[]{:S(2)}) async-start(), calls=%async_computation.2 | async-start | bytes 4259840 | tf_op jit(solution)/shard_map/all_gather | solution.py:72
Sparse Core Ops, SparseCore 0:
  18.9 150.9 reduce-scatter.1
  362.2 74.8 all-gather.1
where the time goes:
time: 455 us; the launch traced here: 454 us
  blocking collectives  337 us (74%)
  waiting for transfers between devices  72 us (16%)
  between operations  15.5 us (3%)
  local copies, waits for them, and re-layouts  14.2 us (3%)
  matrix products  10.3 us (2%)
    psum x1, blocking collectives, body(): small_gradient = lax.psum(local_small, ('shard', 'section'))  247 us
    psum x1, blocking collectives, body(): big_total = lax.psum(owned_squares, ('shard', 'tensor', 'section'))  81.1 us
    all_gather x1, waiting for transfers between devices, body(): lax.all_gather(owned_weights, ('shard', 'section'), axis=0, tiled=True)  72 us
    unnamed x20, local copies, waits for them, and re-layouts  14.2 us
    dot_general x1, matrix products, body(): jnp.einsum('tf,tjc->fjc', normed_inputs, projection_cotangent, preferred_...  10.3 us
    psum x1, blocking collectives, body(): small_total = lax.psum(jnp.sum(small_gradient * small_gradient), 'tensor')  9.45 us
  transfers between devices with their start and end apart: 2, of which 1 were waited for; matrix products, arithmetic and copies ran while one was open for 1% of the time, Pallas kernels for 0%

commit v1 on v0

v1 whole, which is shorter than its diff:
```python
import functools
import math

import jax
import jax.numpy as jnp
from jax import lax
from jax.experimental import pallas as pl
from jax.experimental.pallas import tpu as pltpu
from jax.sharding import PartitionSpec as P

D = 4096
EXPERTS = 8
STEP = 10
KV_COLS = 1024
SMALL_ROWS = 10

beta_one = 0.9
beta_two = 0.95
learning_rate = 0.01
weight_decay = 0.1
epsilon = 1e-08
clip_factor = 0.5

F32 = jnp.float32
BF16 = jnp.bfloat16
MESH = pl.DeviceIdType.MESH

ROWS = 64
HALF = 256
Z_FIRST = 16
LAST_Z = 96


def adamw(gradient, scale, first, second, master, decay):
    clipped = gradient * scale
    first_new = beta_one * first + (1.0 - beta_one) * clipped
    second_new = beta_two * second + (1.0 - beta_two) * clipped * clipped
    first_hat = first_new / (1.0 - beta_one**STEP)
    second_hat = second_new / (1.0 - beta_two**STEP)
    master_new = master - learning_rate * (
        first_hat / (jnp.sqrt(second_hat) + epsilon) + decay * master
    )
    return (master_new, first_new, second_new)


def folded(square):
    return square.reshape(-1, 8, 128).sum(axis=0)


def kernel(
    ny, nx, nz,
    g, small, mw, m1, m2, sm, s1, s2,
    om, o1, o2, gat, osm, os1, os2, osw,
    pair, za, yb, ra, rb, sy, ry, sz, szf, rz, own_grad,
    smz, smr, smc, smy, smf, nzs, ncs, nys, nxs,
    pair_s, pair_r, za_s, za_r, yb_s, yb_r, sy_s, sy_r, sz_s, sz_r,
    smz_s, smz_r, smc_s, smc_r, smy_s, smy_r, smf_s, smf_r,
    nz_s, nz_r, nc_s, nc_r, ny_s, ny_r, nx_s, nx_r,
    a1_s, a1_r, b1_s, b1_r, a2_s, a2_r, b2_s, b2_r, fa_s, fa_r, fb_s, fb_r,
):
    shard = lax.axis_index("shard")
    x = lax.axis_index("tensor")
    z = lax.axis_index("section")
    y, c = shard // 2, shard % 2
    other = 1 - c
    sibling = (y * 2 + other, x, z)

    def at_y(d):
        yy = (y + d) % ny
        return yy, (yy * 2 + c, x, z)

    def at_z(d):
        zz = (z + d) % nz
        return zz, (shard, x, zz)

    def at_x(d):
        xx = (x + d) % nx
        return xx, (shard, xx, z)

    def copy(src, dst, send, recv, device):
        return pltpu.make_async_remote_copy(
            src_ref=src, dst_ref=dst, send_sem=send, recv_sem=recv, device_id=device, device_id_type=MESH
        )

    sent = []

    def send(*a):
        made = copy(*a)
        made.start()
        sent.append(made)

    barrier = pltpu.get_barrier_semaphore()
    peers = [sibling] + [at_y(d)[1] for d in range(1, ny)] + [at_z(d)[1] for d in range(1, nz)] + [at_x(d)[1] for d in range(1, nx)]
    for peer in peers:
        pl.semaphore_signal(barrier, inc=1, device_id=peer, device_id_type=MESH)
    pl.semaphore_wait(barrier, len(peers))

    for d in list(range(1, ny)) + [0]:
        yy, _ = at_y(d)
        send(g.at[:, yy, other], pair.at[:, yy], pair_s.at[d], pair_r.at[yy], sibling)

    smz[...] = jnp.zeros_like(smz)
    for i in range(nz):
        smz[i, 0:SMALL_ROWS, :] = small[:, i * 128 : (i + 1) * 128].astype(F32)
    smr[z] = smz[z]
    for d in range(1, nz):
        zz, peer = at_z(d)
        send(smz.at[zz], smr.at[z], smz_s.at[d], smz_r.at[z], peer)

    for d in list(range(1, ny)) + [0]:
        yy, peer = at_y(d)
        copy(g.at[:, yy, other], pair.at[:, yy], pair_s.at[d], pair_r.at[yy], sibling).wait_recv()

        def add(i, carry, yy=yy):
            j, zz = i // nz, i % nz
            both = (g[j, yy, c, zz].astype(F32) + pair[j, yy, zz].astype(F32)).astype(BF16)
            za[zz, j, yy] = both[0:Z_FIRST]
            yb[yy, j, zz] = both[Z_FIRST:ROWS]
            return carry

        lax.fori_loop(0, 2 * nz, add, 0)
        if d:
            send(yb.at[yy], rb.at[y], yb_s.at[d], yb_r.at[y], peer)
    for d in range(1, nz):
        zz, peer = at_z(d)
        send(za.at[zz], ra.at[z], za_s.at[d], za_r.at[z], peer)

    for d in range(1, nz):
        zz, peer = at_z(d)
        copy(smz.at[zz], smr.at[zz], smz_s.at[d], smz_r.at[zz], peer).wait_recv()
    block = smr[0]
    for i in range(1, nz):
        block = block + smr[i]
    smc[c] = block
    send(smc.at[c], smc.at[c], smc_s.at[0], smc_r.at[c], sibling)

    for d in range(1, nz):
        zz, peer = at_z(d)
        copy(za.at[zz], ra.at[zz], za_s.at[d], za_r.at[zz], peer).wait_recv()

    def sum_z(i, carry):
        j, yy = i // ny, i % ny
        total = g[j, yy, c, z, 0:Z_FIRST].astype(F32) + pair[j, yy, z, 0:Z_FIRST].astype(F32)
        for d in range(1, nz):
            total = total + ra[(z + d) % nz, j, yy].astype(F32)
        sy[yy, j] = total
        return carry

    lax.fori_loop(0, 2 * ny, sum_z, 0)
    for d in range(1, ny):
        yy, peer = at_y(d)
        send(sy.at[yy], ry.at[y], sy_s.at[d], sy_r.at[y], peer)

    copy(smc.at[c], smc.at[other], smc_s.at[0], smc_r.at[other], sibling).wait_recv()
    smy[y] = smc[0] + smc[1]
    for d in range(1, ny):
        yy, peer = at_y(d)
        send(smy.at[y], smy.at[y], smy_s.at[d], smy_r.at[y], peer)

    for d in range(1, ny):
        yy, peer = at_y(d)
        copy(yb.at[yy], rb.at[yy], yb_s.at[d], yb_r.at[yy], peer).wait_recv()

    def sum_y(i, carry):
        j, zz = i // nz, i % nz
        total = g[j, y, c, zz, Z_FIRST:ROWS].astype(F32) + pair[j, y, zz, Z_FIRST:ROWS].astype(F32)
        for d in range(1, ny):
            total = total + rb[(y + d) % ny, j, zz].astype(F32)
        szf[zz, j] = total
        sz[zz, j] = total.astype(BF16)
        return carry

    lax.fori_loop(0, 2 * nz, sum_y, 0)
    for d in range(1, nz):
        zz, peer = at_z(d)
        send(sz.at[zz], rz.at[z], sz_s.at[d], sz_r.at[z], peer)

    for d in range(1, ny):
        yy, peer = at_y(d)
        copy(smy.at[y], smy.at[yy], smy_s.at[d], smy_r.at[yy], peer).wait_recv()
    block = smy[0]
    for i in range(1, ny):
        block = block + smy[i]
    smf[z] = block
    for d in range(1, nz):
        zz, peer = at_z(d)
        send(smf.at[z], smf.at[z], smf_s.at[d], smf_r.at[z], peer)

    for d in range(1, ny):
        yy, peer = at_y(d)
        copy(sy.at[yy], ry.at[yy], sy_s.at[d], sy_r.at[yy], peer).wait_recv()
    for j in range(2):
        total = sy[y, j]
        for d in range(1, ny):
            total = total + ry[(y + d) % ny, j]
        for q in range(2):
            own_grad[pl.ds(2 * q + j, Z_FIRST, stride=4), :] = total[:, q * 128 : (q + 1) * 128]
    for d in range(1, nz):
        zz, peer = at_z(d)
        copy(sz.at[zz], rz.at[zz], sz_s.at[d], sz_r.at[zz], peer).wait_recv()
    for j in range(2):
        total = szf[z, j]
        for d in range(1, nz):
            total = total + rz[(z + d) % nz, j].astype(F32)
        for q in range(2):
            own_grad[pl.ds(4 * Z_FIRST + 2 * q + j, ROWS - Z_FIRST, stride=4), :] = total[:, q * 128 : (q + 1) * 128]

    grad = own_grad[...]
    nzs[z] = folded(grad * grad)
    for d in range(1, nz):
        zz, peer = at_z(d)
        send(nzs.at[z], nzs.at[z], nz_s.at[d], nz_r.at[z], peer)
    for d in range(1, nz):
        zz, peer = at_z(d)
        copy(smf.at[z], smf.at[zz], smf_s.at[d], smf_r.at[zz], peer).wait_recv()
    small_square = jnp.zeros((8, 128), F32)
    for i in range(nz):
        rows = smf[i]
        small_square = small_square + folded(rows * rows)
    for d in range(1, nz):
        zz, peer = at_z(d)
        copy(nzs.at[z], nzs.at[zz], nz_s.at[d], nz_r.at[zz], peer).wait_recv()
    part = nzs[0]
    for i in range(1, nz):
        part = part + nzs[i]
    ncs[c] = part
    send(ncs.at[c], ncs.at[c], nc_s.at[0], nc_r.at[c], sibling)
    copy(ncs.at[c], ncs.at[other], nc_s.at[0], nc_r.at[other], sibling).wait_recv()
    nys[y] = ncs[0] + ncs[1]
    for d in range(1, ny):
        yy, peer = at_y(d)
        send(nys.at[y], nys.at[y], ny_s.at[d], ny_r.at[y], peer)
    for d in range(1, ny):
        yy, peer = at_y(d)
        copy(nys.at[y], nys.at[yy], ny_s.at[d], ny_r.at[yy], peer).wait_recv()
    part = small_square
    for i in range(ny):
        part = part + nys[i]
    nxs[x] = part
    for d in range(1, nx):
        xx, peer = at_x(d)
        send(nxs.at[x], nxs.at[x], nx_s.at[d], nx_r.at[x], peer)
    for d in range(1, nx):
        xx, peer = at_x(d)
        copy(nxs.at[x], nxs.at[xx], nx_s.at[d], nx_r.at[xx], peer).wait_recv()
    part = nxs[0]
    for i in range(1, nx):
        part = part + nxs[i]
    total = jnp.sum(part, keepdims=True)
    limit = clip_factor * math.sqrt(2 * D * KV_COLS + SMALL_ROWS * D)
    scale = jnp.minimum(1.0, limit / (jnp.sqrt(total) + 1e-06))

    master_new, first_new, second_new = adamw(grad, scale, m1[...], m2[...], mw[...], weight_decay)
    gat[y, c, z] = master_new.astype(BF16)

    for d in range(1, nz):
        zz, peer = at_z(d)
        part = gat.at[y, c, z, LAST_Z:256]
        send(part, part, b1_s.at[d], b1_r.at[z], peer)
    for d in range(1, ny):
        yy, peer = at_y(d)
        part = gat.at[y, c, z, 0:LAST_Z]
        send(part, part, a1_s.at[d], a1_r.at[y], peer)

    om[...] = master_new
    o1[...] = first_new
    o2[...] = second_new
    decay = jnp.where(lax.broadcasted_iota(jnp.int32, (SMALL_ROWS, 128), 0) < EXPERTS, weight_decay, 0.0).astype(F32)
    for i in range(nz):
        lanes = slice(i * 128, (i + 1) * 128)
        made = adamw(smf[i, 0:SMALL_ROWS, :], scale, s1[:, lanes], s2[:, lanes], sm[:, lanes], decay)
        osm[:, lanes], os1[:, lanes], os2[:, lanes] = made
        osw[:, lanes] = made[0].astype(BF16)

    def z_block(core, zz):
        return gat.at[:, core, zz, 0:LAST_Z]

    def y_block(core, yy):
        return gat.at[yy, core, :, LAST_Z:256]

    for d in range(1, ny):
        yy, peer = at_y(d)
        part = gat.at[yy, c, z, 0:LAST_Z]
        copy(part, part, a1_s.at[d], a1_r.at[yy], peer).wait_recv()
    for d in range(1, nz):
        zz, peer = at_z(d)
        send(z_block(c, z), z_block(c, z), a2_s.at[d], a2_r.at[z], peer)
    send(z_block(c, z), z_block(c, z), fa_s.at[0], fa_r.at[z], sibling)
    for d in range(1, nz):
        zz, peer = at_z(d)
        part = gat.at[y, c, zz, LAST_Z:256]
        copy(part, part, b1_s.at[d], b1_r.at[zz], peer).wait_recv()
    for d in range(1, ny):
        yy, peer = at_y(d)
        send(y_block(c, y), y_block(c, y), b2_s.at[d], b2_r.at[y], peer)
    send(y_block(c, y), y_block(c, y), fb_s.at[0], fb_r.at[y], sibling)

    def on_z(d):
        zz, peer = at_z(d)
        copy(z_block(c, zz), z_block(c, zz), a2_s.at[d], a2_r.at[zz], peer).wait_recv()
        send(z_block(c, zz), z_block(c, zz), fa_s.at[d], fa_r.at[zz], sibling)

    def on_y(d):
        yy, peer = at_y(d)
        copy(y_block(c, yy), y_block(c, yy), b2_s.at[d], b2_r.at[yy], peer).wait_recv()
        send(y_block(c, yy), y_block(c, yy), fb_s.at[d], fb_r.at[yy], sibling)

    near = sorted(range(1, nz), key=lambda d: min(d, nz - d))
    near_y = sorted(range(1, ny), key=lambda d: min(d, ny - d))
    for d in near:
        on_z(d)
        if near_y:
            on_y(near_y.pop(0))
    for d in range(nz):
        zz, _ = at_z(d)
        copy(z_block(c, zz), z_block(other, zz), fa_s.at[d], fa_r.at[zz], sibling).wait_recv()
    for d in range(ny):
        yy, _ = at_y(d)
        copy(y_block(c, yy), y_block(other, yy), fb_s.at[d], fb_r.at[yy], sibling).wait_recv()
    for made in sent:
        made.wait_send()


def stored(array):
    rows = array.shape[0]
    return array.reshape(rows, 2, 2, 128).transpose(0, 2, 1, 3).reshape(rows * 4, 128)


def unstored(array):
    rows = array.shape[0] // 4
    return array.reshape(rows, 2, 2, 128).transpose(0, 2, 1, 3).reshape(rows, 2, 256)


def body(
    ny, nx, nz,
    normed_inputs,
    projection_cotangent,
    small_partials,
    master_weights,
    first_moment,
    second_moment,
    small_master,
    small_first,
    small_second,
):
    gradient = jnp.einsum(
        "tf,tjc->fjc", normed_inputs, projection_cotangent, preferred_element_type=F32
    ).astype(BF16).transpose(1, 0, 2)
    features = gradient.shape[1]
    assert features == ny * 2 * nz * ROWS
    gradient = gradient.reshape(2, ny, 2, nz, ROWS, HALF)
    small_shape = jax.ShapeDtypeStruct(small_master.shape, F32)
    owned = jax.ShapeDtypeStruct((4 * ROWS, 128), F32)
    dma = pltpu.SemaphoreType.DMA
    vm = pltpu.VMEM
    last = ROWS - Z_FIRST
    along_y, along_z, along_x = [dma((ny,))] * 2, [dma((nz,))] * 2, [dma((nx,))] * 2
    pairs = [dma((2,))] * 2
    outs = pl.pallas_call(
        functools.partial(kernel, ny, nx, nz),
        out_shape=(
            owned, owned, owned,
            jax.ShapeDtypeStruct((ny, 2, nz, 4 * ROWS, 128), BF16),
            small_shape, small_shape, small_shape,
            jax.ShapeDtypeStruct(small_master.shape, BF16),
        ),
        in_specs=[pl.BlockSpec(memory_space=pltpu.VMEM)] * 8,
        out_specs=[pl.BlockSpec(memory_space=pltpu.VMEM)] * 8,
        scratch_shapes=[
            vm((2, ny, nz, ROWS, HALF), BF16),
            vm((nz, 2, ny, Z_FIRST, HALF), BF16),
            vm((ny, 2, nz, last, HALF), BF16),
            vm((nz, 2, ny, Z_FIRST, HALF), BF16),
            vm((ny, 2, nz, last, HALF), BF16),
            vm((ny, 2, Z_FIRST, HALF), F32),
            vm((ny, 2, Z_FIRST, HALF), F32),
            vm((nz, 2, last, HALF), BF16),
            vm((nz, 2, last, HALF), F32),
            vm((nz, 2, last, HALF), BF16),
            vm((4 * ROWS, 128), F32),
            vm((nz, 16, 128), F32),
            vm((nz, 16, 128), F32),
            vm((2, 16, 128), F32),
            vm((ny, 16, 128), F32),
            vm((nz, 16, 128), F32),
            vm((nz, 8, 128), F32),
            vm((2, 8, 128), F32),
            vm((ny, 8, 128), F32),
            vm((nx, 8, 128), F32),
            *along_y, *along_z, *along_y, *along_y, *along_z,
            *along_z, *pairs, *along_y, *along_z,
            *along_z, *pairs, *along_y, *along_x,
            *along_y, *along_z, *along_z, *along_y, *along_z, *along_y,
        ],
        compiler_params=pltpu.CompilerParams(
            collective_id=0, has_side_effects=True, vmem_limit_bytes=48 << 20
        ),
    )(
        gradient, small_partials[0], stored(master_weights), stored(first_moment), stored(second_moment),
        small_master, small_first, small_second,
    )
    return (
        unstored(outs[0]), unstored(outs[1]), unstored(outs[2]),
        unstored(outs[3].reshape(-1, 128)),
        outs[4], outs[5], outs[6], outs[7],
    )


def solution(mesh):
    ny, nx, nz = mesh.shape["shard"] // 2, mesh.shape["tensor"], mesh.shape["section"]
    rows = P(("shard", "section"), None, "tensor")
    flat = P(None, "tensor")
    return jax.shard_map(
        functools.partial(body, ny, nx, nz),
        mesh=mesh,
        in_specs=(P(("shard", "section"), None), rows, rows, rows, rows, rows, flat, flat, flat),
        out_specs=(rows, rows, rows, P(None, None, "tensor"), flat, flat, flat, flat),
        check_vma=False,
    )
```

time: 455 us -> 109 us (0.24)
  blocking collectives: 337 us -> 0 us
  Pallas kernels: 0 us -> 90.5 us
  waiting for transfers between devices: 72 us -> 0 us
  between operations: 15.5 us -> 0.72 us
  local copies, waits for them, and re-layouts: 14.2 us -> 7.73 us
    psum x3 -> x0, blocking collectives: 337 us -> none  [the longest x1 247 us: body(): small_gradient = lax.psum(local_small, ('shard', 'section'))]
    pallas_call x0 -> x1, Pallas kernels: none -> 90.5 us  [body(): pl.pallas_call(functools.partial(kernel, ny, nx, nz), out_shape=(owned, o...]
    all_gather x1 -> x0, waiting for transfers between devices: 72 us -> none  [body(): lax.all_gather(owned_weights, ('shard', 'section'), axis=0, tiled=True)]
    unnamed x20 -> x24, local copies, waits for them, and re-layouts: 14.2 us -> 7.73 us
  transfers between devices with their start and end apart: 2 -> 0, of which waited for: 1 -> 0; matrix products, arithmetic and copies ran while one was open for 1% -> 0% of each run, Pallas kernels for 0% -> 0%
where the time goes in v1:
time: 109 us
  Pallas kernels  90.5 us (83%)
  matrix products  9.85 us (9%)
  local copies, waits for them, and re-layouts  7.73 us (7%)
    pallas_call x1, Pallas kernels, body(): pl.pallas_call(functools.partial(kernel, ny, nx, nz), out_shape=(owned, o...  90.5 us
    dot_general x1, matrix products, body(): jnp.einsum('tf,tjc->fjc', normed_inputs, projection_cotangent, preferred_...  9.85 us
    unnamed x24, local copies, waits for them, and re-layouts  7.73 us

profile of v1, /device:TPU:1, one launch (start us, length us, event | category | flops | bytes accessed | tf_op | source)
XLA Modules:
  0.0 108.8 jit_solution(9099537924812067431)
XLA Ops:
  0.6 0.0 copy-start
  0.7 1.2 %copy-done = bf16[1024,2,256]{2,1,0:T(2,128)(2,1)S(1)} copy-done((bf16[1024,2,256]{2,1,0:T(2,128)(2,1)S(1)}, bf16[1024,2,256]{2,1,0:T(2,128)(2,1)}, u32[]{:S(2)}) %copy-start) | copy-done | bytes 1048600
  1.9 0.0 copy-start.1
  1.9 0.0 copy-start.2
  1.9 0.0 copy-start.5
  1.9 0.0 copy-start.6
  1.9 0.0 copy-start.7
  1.9 9.8 %fusion.2 = bf16[4096,2,256]{2,0,1:T(8,128)(2,1)} fusion(bf16[1024,4096]{1,0:T(8,128)(2,1)} %param.9, bf16[1024,2,256]{2,1,0:T(2,128)(2,1)S(1)} %copy-done), kind=kOutput, calls=%fused_computation.2 | convolution fusion | flops 4297064448 | bytes 13631488 | tf_op jit(solution)/shard_map/tf,tjc->fjc/dot_general | solution.py:346
  11.8 0.0 copy-done.1
  11.8 0.0 copy-done.2
  11.8 0.0 copy-done.3
  11.8 0.0 copy-done.4
  11.8 0.0 copy-done.5
  11.8 0.0 copy-done.6
  11.8 0.0 copy-done.7
  11.8 90.5 %shard_map.152 = (f32[256,128]{1,0:T(8,128)S(1)}, f32[256,128]{1,0:T(8,128)S(1)}, f32[256,128]{1,0:T(8,128)S(1)}, bf16[4,2,8,256,128]{4,3,2,1,0:T(8,128)(2,1)S(1...) custom-call(bf16[2,4,2,8,64,256]{5,4,3,2,1,0:T(8,128)(2,1)} %bitcast, ...), custom_call_target="tpu_custom_call" | custom-call | tf_op jit(solution)/shard_map/pallas_call | solution.py:359
  102.3 0.7 copy.38
  103.0 0.7 copy.39
  103.7 0.7 copy.40
  104.3 2.0 %copy.41 = bf16[4096,2,256]{2,1,0:T(2,128)(2,1)} copy(bf16[4096,2,256]{2,1,0:T(2,128)(2,1)S(1)} %bitcast.44) | data formatting | bytes 8388608
  106.3 0.6 copy.42
  107.0 0.6 copy.43
  107.6 0.6 copy.44
  108.2 0.6 copy.45
  (2 shorter events, 0.0 us)
Async XLA Ops:
  0.6 1.2 %copy-start = (bf16[1024,2,256]{2,1,0:T(2,128)(2,1)S(1)}, bf16[1024,2,256]{2,1,0:T(2,128)(2,1)}, u32[]{:S(2)}) copy-start(bf16[1024,2,256]{2,1,0:T(2,128)(2,1)} %param.10) | copy-start | bytes 3145732
  1.9 9.9 %copy-start.1 = (f32[64,2,256]{2,1,0:T(2,128)S(1)}, f32[64,2,256]{2,1,0:T(2,128)}, u32[]{:S(2)}) copy-start(f32[64,2,256]{2,1,0:T(2,128)} %param.12) | copy-start | bytes 393220
  1.9 9.9 %copy-start.2 = (f32[64,2,256]{2,1,0:T(2,128)S(1)}, f32[64,2,256]{2,1,0:T(2,128)}, u32[]{:S(2)}) copy-start(f32[64,2,256]{2,1,0:T(2,128)} %param.13) | copy-start | bytes 393220
  1.9 9.9 %copy-start.3 = (f32[64,2,256]{2,1,0:T(2,128)S(1)}, f32[64,2,256]{2,1,0:T(2,128)}, u32[]{:S(2)}) copy-start(f32[64,2,256]{2,1,0:T(2,128)} %param.14) | copy-start | bytes 393220
  1.9 9.9 %copy-start.4 = (f32[10,1024]{1,0:T(8,128)S(1)}, f32[10,1024]{1,0:T(8,128)}, u32[]{:S(2)}) copy-start(f32[10,1024]{1,0:T(8,128)} %sm.1) | copy-start | bytes 122884
  1.9 9.9 %copy-start.5 = (f32[10,1024]{1,0:T(8,128)S(1)}, f32[10,1024]{1,0:T(8,128)}, u32[]{:S(2)}) copy-start(f32[10,1024]{1,0:T(8,128)} %s1_.1) | copy-start | bytes 122884
  1.9 9.9 %copy-start.6 = (f32[10,1024]{1,0:T(8,128)S(1)}, f32[10,1024]{1,0:T(8,128)}, u32[]{:S(2)}) copy-start(f32[10,1024]{1,0:T(8,128)} %s2_.1) | copy-start | bytes 122884
  1.9 9.9 %copy-start.7 = (bf16[1,10,1024]{2,1,0:T(8,128)(2,1)S(1)}, bf16[1,10,1024]{2,1,0:T(8,128)(2,1)}, u32[]{:S(2)}) copy-start(bf16[1,10,1024]{2,1,0:T(8,128)(2,1)} %param.11) | copy-start | bytes 61444

commit v2 on v1

--- a/solution.py
+++ b/solution.py
@@ -27,8 +27,8 @@
 
 ROWS = 64
 HALF = 256
-Z_FIRST = 16
-LAST_Z = 96
+Z_FIRST = 32
+LAST_Z = 128
 
 
 def adamw(gradient, scale, first, second, master, decay):
@@ -51,12 +51,12 @@
     ny, nx, nz,
     g, small, mw, m1, m2, sm, s1, s2,
     om, o1, o2, gat, osm, os1, os2, osw,
-    pair, za, yb, ra, rb, sy, ry, sz, szf, rz, own_grad,
-    smz, smr, smc, smy, smf, nzs, ncs, nys, nxs,
-    pair_s, pair_r, za_s, za_r, yb_s, yb_r, sy_s, sy_r, sz_s, sz_r,
+    pair, zc, zr, yb, rb, sy, ry, sz, szf, rz, own_grad,
+    smz, smr, smc, smy, smf, nzc, nyx,
+    pair_s, pair_r, zc_s, zc_r, yb_s, yb_r, sy_s, sy_r, sz_s, sz_r,
     smz_s, smz_r, smc_s, smc_r, smy_s, smy_r, smf_s, smf_r,
-    nz_s, nz_r, nc_s, nc_r, ny_s, ny_r, nx_s, nx_r,
-    a1_s, a1_r, b1_s, b1_r, a2_s, a2_r, b2_s, b2_r, fa_s, fa_r, fb_s, fb_r,
+    nzc_s, nzc_r, nyx_s, nyx_r,
+    a1_s, a1_r, b1_s, b1_r, gc_s, gc_r, b2_s, b2_r, fa_s, fa_r, fb_s, fb_r,
 ):
     shard = lax.axis_index("shard")
     x = lax.axis_index("tensor")
@@ -73,9 +73,13 @@
         zz = (z + d) % nz
         return zz, (shard, x, zz)
 
-    def at_x(d):
-        xx = (x + d) % nx
-        return xx, (shard, xx, z)
+    def at_zc(d):
+        zz, cc = (z + d // 2) % nz, (c + d % 2) % 2
+        return zz * 2 + cc, (y * 2 + cc, x, zz)
+
+    def at_yx(d):
+        yy, xx = (y + d // nx) % ny, (x + d % nx) % nx
+        return yy * nx + xx, (yy * 2 + c, xx, z)
 
     def copy(src, dst, send, recv, device):
         return pltpu.make_async_remote_copy(
@@ -90,7 +94,7 @@
         sent.append(made)
 
     barrier = pltpu.get_barrier_semaphore()
-    peers = [sibling] + [at_y(d)[1] for d in range(1, ny)] + [at_z(d)[1] for d in range(1, nz)] + [at_x(d)[1] for d in range(1, nx)]
+    peers = [at_zc(d)[1] for d in range(1, 2 * nz)] + [at_yx(d)[1] for d in range(1, ny * nx)]
     for peer in peers:
         pl.semaphore_signal(barrier, inc=1, device_id=peer, device_id_type=MESH)
     pl.semaphore_wait(barrier, len(peers))
@@ -113,18 +117,32 @@
 
         def add(i, carry, yy=yy):
             j, zz = i // nz, i % nz
-            both = (g[j, yy, c, zz].astype(F32) + pair[j, yy, zz].astype(F32)).astype(BF16)
-            za[zz, j, yy] = both[0:Z_FIRST]
-            yb[yy, j, zz] = both[Z_FIRST:ROWS]
+            rows = slice(Z_FIRST, ROWS)
+            both = (g[j, yy, c, zz, rows].astype(F32) + pair[j, yy, zz, rows].astype(F32)).astype(BF16)
+            yb[yy, j, zz] = both
             return carry
 
         lax.fori_loop(0, 2 * nz, add, 0)
         if d:
             send(yb.at[yy], rb.at[y], yb_s.at[d], yb_r.at[y], peer)
-    for d in range(1, nz):
-        zz, peer = at_z(d)
-        send(za.at[zz], ra.at[z], za_s.at[d], za_r.at[z], peer)
-
+    def own_z(j, zz):
+        rows = slice(0, Z_FIRST)
+        return g[j, :, c, zz, rows].astype(F32) + pair[j, :, zz, rows].astype(F32)
+
+    hops = {(j, way): nz // 2 - (j ^ way) for j in range(2) for way in range(2)}
+
+    def step_z(j, way, k):
+        sign = 1 if way == 0 else nz - 1
+        if k:
+            copy(zc.at[j, way, k - 1], zr.at[j, way, k - 1], zc_s.at[j, way, k - 1], zc_r.at[j, way, k - 1], at_z(sign)[1]).wait_recv()
+        total = own_z(j, (z + sign * (hops[j, way] - k)) % nz)
+        if k:
+            total = total + zr[j, way, k - 1].astype(F32)
+        zc[j, way, k] = total.astype(BF16)
+        send(zc.at[j, way, k], zr.at[j, way, k], zc_s.at[j, way, k], zc_r.at[j, way, k], at_z(sign)[1])
+
+    for j, way in hops:
+        step_z(j, way, 0)
     for d in range(1, nz):
         zz, peer = at_z(d)
         copy(smz.at[zz], smr.at[zz], smz_s.at[d], smz_r.at[zz], peer).wait_recv()
@@ -134,19 +152,18 @@
     smc[c] = block
     send(smc.at[c], smc.at[c], smc_s.at[0], smc_r.at[c], sibling)
 
-    for d in range(1, nz):
-        zz, peer = at_z(d)
-        copy(za.at[zz], ra.at[zz], za_s.at[d], za_r.at[zz], peer).wait_recv()
-
-    def sum_z(i, carry):
-        j, yy = i // ny, i % ny
-        total = g[j, yy, c, z, 0:Z_FIRST].astype(F32) + pair[j, yy, z, 0:Z_FIRST].astype(F32)
-        for d in range(1, nz):
-            total = total + ra[(z + d) % nz, j, yy].astype(F32)
-        sy[yy, j] = total
-        return carry
-
-    lax.fori_loop(0, 2 * ny, sum_z, 0)
+    for k in range(1, nz // 2):
+        for j, way in hops:
+            if k < hops[j, way]:
+                step_z(j, way, k)
+    for j in range(2):
+        total = own_z(j, z)
+        for way in range(2):
+            k = hops[j, way] - 1
+            peer = at_z(1 if way == 0 else nz - 1)[1]
+            copy(zc.at[j, way, k], zr.at[j, way, k], zc_s.at[j, way, k], zc_r.at[j, way, k], peer).wait_recv()
+            total = total + zr[j, way, k].astype(F32)
+        sy[:, j] = total
     for d in range(1, ny):
         yy, peer = at_y(d)
         send(sy.at[yy], ry.at[y], sy_s.at[d], sy_r.at[y], peer)
@@ -206,10 +223,11 @@
             own_grad[pl.ds(4 * Z_FIRST + 2 * q + j, ROWS - Z_FIRST, stride=4), :] = total[:, q * 128 : (q + 1) * 128]
 
     grad = own_grad[...]
-    nzs[z] = folded(grad * grad)
-    for d in range(1, nz):
-        zz, peer = at_z(d)
-        send(nzs.at[z], nzs.at[z], nz_s.at[d], nz_r.at[z], peer)
+    here = z * 2 + c
+    nzc[here] = folded(grad * grad)
+    for d in range(1, 2 * nz):
+        there, peer = at_zc(d)
+        send(nzc.at[here], nzc.at[here], nzc_s.at[d], nzc_r.at[here], peer)
     for d in range(1, nz):
         zz, peer = at_z(d)
         copy(smf.at[z], smf.at[zz], smf_s.at[d], smf_r.at[zz], peer).wait_recv()
@@ -217,35 +235,23 @@
     for i in range(nz):
         rows = smf[i]
         small_square = small_square + folded(rows * rows)
-    for d in range(1, nz):
-        zz, peer = at_z(d)
-        copy(nzs.at[z], nzs.at[zz], nz_s.at[d], nz_r.at[zz], peer).wait_recv()
-    part = nzs[0]
-    for i in range(1, nz):
-        part = part + nzs[i]
-    ncs[c] = part
-    send(ncs.at[c], ncs.at[c], nc_s.at[0], nc_r.at[c], sibling)
-    copy(ncs.at[c], ncs.at[other], nc_s.at[0], nc_r.at[other], sibling).wait_recv()
-    nys[y] = ncs[0] + ncs[1]
-    for d in range(1, ny):
-        yy, peer = at_y(d)
-        send(nys.at[y], nys.at[y], ny_s.at[d], ny_r.at[y], peer)
-    for d in range(1, ny):
-        yy, peer = at_y(d)
-        copy(nys.at[y], nys.at[yy], ny_s.at[d], ny_r.at[yy], peer).wait_recv()
-    part = small_square
-    for i in range(ny):
-        part = part + nys[i]
-    nxs[x] = part
-    for d in range(1, nx):
-        xx, peer = at_x(d)
-        send(nxs.at[x], nxs.at[x], nx_s.at[d], nx_r.at[x], peer)
-    for d in range(1, nx):
-        xx, peer = at_x(d)
-        copy(nxs.at[x], nxs.at[xx], nx_s.at[d], nx_r.at[xx], peer).wait_recv()
-    part = nxs[0]
-    for i in range(1, nx):
-        part = part + nxs[i]
+    for d in range(1, 2 * nz):
+        there, peer = at_zc(d)
+        copy(nzc.at[here], nzc.at[there], nzc_s.at[d], nzc_r.at[there], peer).wait_recv()
+    part = small_square * (1.0 / ny)
+    for i in range(2 * nz):
+        part = part + nzc[i]
+    here = y * nx + x
+    nyx[here] = part
+    for d in range(1, ny * nx):
+        there, peer = at_yx(d)
+        send(nyx.at[here], nyx.at[here], nyx_s.at[d], nyx_r.at[here], peer)
+    for d in range(1, ny * nx):
+        there, peer = at_yx(d)
+        copy(nyx.at[here], nyx.at[there], nyx_s.at[d], nyx_r.at[there], peer).wait_recv()
+    part = nyx[0]
+    for i in range(1, ny * nx):
+        part = part + nyx[i]
     total = jnp.sum(part, keepdims=True)
     limit = clip_factor * math.sqrt(2 * D * KV_COLS + SMALL_ROWS * D)
     scale = jnp.minimum(1.0, limit / (jnp.sqrt(total) + 1e-06))
@@ -272,8 +278,8 @@
         osm[:, lanes], os1[:, lanes], os2[:, lanes] = made
         osw[:, lanes] = made[0].astype(BF16)
 
-    def z_block(core, zz):
-        return gat.at[:, core, zz, 0:LAST_Z]
+    def z_block(core, zz, half):
+        return gat.at[:, core, zz, half * (LAST_Z // 2) : (half + 1) * (LAST_Z // 2)]
 
     def y_block(core, yy):
         return gat.at[yy, core, :, LAST_Z:256]
@@ -282,10 +288,20 @@
         yy, peer = at_y(d)
         part = gat.at[yy, c, z, 0:LAST_Z]
         copy(part, part, a1_s.at[d], a1_r.at[yy], peer).wait_recv()
-    for d in range(1, nz):
-        zz, peer = at_z(d)
-        send(z_block(c, z), z_block(c, z), a2_s.at[d], a2_r.at[z], peer)
-    send(z_block(c, z), z_block(c, z), fa_s.at[0], fa_r.at[z], sibling)
+
+    def step_g(half, way, k):
+        sign = 1 if way == 0 else nz - 1
+        zz = (z + (nz - sign) * k) % nz
+        part = z_block(c, zz, half)
+        if k:
+            copy(part, part, gc_s.at[half, way, k - 1], gc_r.at[half, way, k - 1], at_z(nz - sign)[1]).wait_recv()
+        if k < hops[half, way]:
+            send(part, part, gc_s.at[half, way, k], gc_r.at[half, way, k], at_z(sign)[1])
+        if k or way == 0:
+            send(part, part, fa_s.at[half, way, k], fa_r.at[half, way, k], sibling)
+
+    for half, way in hops:
+        step_g(half, way, 0)
     for d in range(1, nz):
         zz, peer = at_z(d)
         part = gat.at[y, c, zz, LAST_Z:256]
@@ -295,30 +311,39 @@
         send(y_block(c, y), y_block(c, y), b2_s.at[d], b2_r.at[y], peer)
     send(y_block(c, y), y_block(c, y), fb_s.at[0], fb_r.at[y], sibling)
 
-    def on_z(d):
-        zz, peer = at_z(d)
-        copy(z_block(c, zz), z_block(c, zz), a2_s.at[d], a2_r.at[zz], peer).wait_recv()
-        send(z_block(c, zz), z_block(c, zz), fa_s.at[d], fa_r.at[zz], sibling)
-
     def on_y(d):
         yy, peer = at_y(d)
         copy(y_block(c, yy), y_block(c, yy), b2_s.at[d], b2_r.at[yy], peer).wait_recv()
         send(y_block(c, yy), y_block(c, yy), fb_s.at[d], fb_r.at[yy], sibling)
 
-    near = sorted(range(1, nz), key=lambda d: min(d, nz - d))
     near_y = sorted(range(1, ny), key=lambda d: min(d, ny - d))
-    for d in near:
-        on_z(d)
-        if near_y:
+    for k in range(1, nz // 2 + 1):
+        for half, way in hops:
+            if k <= hops[half, way]:
+                step_g(half, way, k)
+        if k >= 2 and near_y:
             on_y(near_y.pop(0))
-    for d in range(nz):
-        zz, _ = at_z(d)
-        copy(z_block(c, zz), z_block(other, zz), fa_s.at[d], fa_r.at[zz], sibling).wait_recv()
+    for d in near_y:
+        on_y(d)
+    for half, way in hops:
+        for k in range(way, hops[half, way] + 1):
+            sign = 1 if way == 0 else nz - 1
+            zz = (z + (nz - sign) * k) % nz
+            copy(z_block(c, zz, half), z_block(other, zz, half), fa_s.at[half, way, k], fa_r.at[half, way, k], sibling).wait_recv()
     for d in range(ny):
         yy, _ = at_y(d)
         copy(y_block(c, yy), y_block(other, yy), fb_s.at[d], fb_r.at[yy], sibling).wait_recv()
     for made in sent:
         made.wait_send()
+
+
+def leave(count, *refs):
+    semaphores = refs[2 * count]
+    copies = [pltpu.make_async_copy(refs[i], refs[count + i], semaphores.at[i]) for i in range(count)]
+    for made in copies:
+        made.start()
+    for made in copies:
+        made.wait()
 
 
 def stored(array):
@@ -354,8 +379,8 @@
     dma = pltpu.SemaphoreType.DMA
     vm = pltpu.VMEM
     last = ROWS - Z_FIRST
-    along_y, along_z, along_x = [dma((ny,))] * 2, [dma((nz,))] * 2, [dma((nx,))] * 2
-    pairs = [dma((2,))] * 2
+    along_y, along_z = [dma((ny,))] * 2, [dma((nz,))] * 2
+    pairs, chains = [dma((2,))] * 2, [dma((2, 2, nz // 2))] * 2
     outs = pl.pallas_call(
         functools.partial(kernel, ny, nx, nz),
         out_shape=(
@@ -368,9 +393,9 @@
         out_specs=[pl.BlockSpec(memory_space=pltpu.VMEM)] * 8,
         scratch_shapes=[
             vm((2, ny, nz, ROWS, HALF), BF16),
-            vm((nz, 2, ny, Z_FIRST, HALF), BF16),
+            vm((2, 2, nz // 2, ny, Z_FIRST, HALF), BF16),
+            vm((2, 2, nz // 2, ny, Z_FIRST, HALF), BF16),
             vm((ny, 2, nz, last, HALF), BF16),
-            vm((nz, 2, ny, Z_FIRST, HALF), BF16),
             vm((ny, 2, nz, last, HALF), BF16),
             vm((ny, 2, Z_FIRST, HALF), F32),
             vm((ny, 2, Z_FIRST, HALF), F32),
@@ -383,14 +408,12 @@
             vm((2, 16, 128), F32),
             vm((ny, 16, 128), F32),
             vm((nz, 16, 128), F32),
-            vm((nz, 8, 128), F32),
-            vm((2, 8, 128), F32),
-            vm((ny, 8, 128), F32),
-            vm((nx, 8, 128), F32),
-            *along_y, *along_z, *along_y, *along_y, *along_z,
+            vm((2 * nz, 8, 128), F32),
+            vm((ny * nx, 8, 128), F32),
+            *along_y, *chains, *along_y, *along_y, *along_z,
             *along_z, *pairs, *along_y, *along_z,
-            *along_z, *pairs, *along_y, *along_x,
-            *along_y, *along_z, *along_z, *along_y, *along_z, *along_y,
+            *[dma((2 * nz,))] * 2, *[dma((ny * nx,))] * 2,
+            *along_y, *along_z, *chains, *along_y, *[dma((2, 2, nz // 2 + 1))] * 2, *along_y,
         ],
         compiler_params=pltpu.CompilerParams(
             collective_id=0, has_side_effects=True, vmem_limit_bytes=48 << 20
@@ -399,6 +422,15 @@
         gradient, small_partials[0], stored(master_weights), stored(first_moment), stored(second_moment),
         small_master, small_first, small_second,
     )
+    count = len(outs)
+    outs = pl.pallas_call(
+        functools.partial(leave, count),
+        out_shape=[jax.ShapeDtypeStruct(o.shape, o.dtype) for o in outs],
+        in_specs=[pl.BlockSpec(memory_space=pltpu.VMEM)] * count,
+        out_specs=[pl.BlockSpec(memory_space=pl.ANY)] * count,
+        scratch_shapes=[dma((count,))],
+        compiler_params=pltpu.CompilerParams(vmem_limit_bytes=16 << 20),
+    )(*outs)
     return (
         unstored(outs[0]), unstored(outs[1]), unstored(outs[2]),
         unstored(outs[3].reshape(-1, 128)),

time: 109 us -> 93.9 us (0.86)
  Pallas kernels: 90.5 us -> 81.9 us
  local copies, waits for them, and re-layouts: 7.73 us -> 1.25 us
    pallas_call x1, Pallas kernels: 90.5 us -> 79.7 us  [body(): pl.pallas_call(functools.partial(kernel, ny, nx, nz), out_shape=(owned, o...]
    unnamed x24 -> x16, local copies, waits for them, and re-layouts: 7.73 us -> 1.25 us
    pallas_call x0 -> x1, Pallas kernels: none -> 2.26 us  [body(): pl.pallas_call(functools.partial(leave, count), out_shape=[jax.ShapeDtype...]
where the time goes in v2:
time: 93.9 us; the launch traced here: 93.8 us
  Pallas kernels  81.9 us (87%)
  matrix products  9.85 us (10%)
  local copies, waits for them, and re-layouts  1.25 us (1%)
    pallas_call x1, Pallas kernels, body(): pl.pallas_call(functools.partial(kernel, ny, nx, nz), out_shape=(owned, o...  79.7 us
    dot_general x1, matrix products, body(): jnp.einsum('tf,tjc->fjc', normed_inputs, projection_cotangent, preferred_...  9.85 us
    pallas_call x1, Pallas kernels, body(): pl.pallas_call(functools.partial(leave, count), out_shape=[jax.ShapeDtype...  2.26 us

profile of v2, /device:TPU:1, one launch (start us, length us, event | category | flops | bytes accessed | tf_op | source)
XLA Modules:
  0.0 93.8 jit_solution(14990828500382027198)
XLA Ops:
  0.6 0.0 copy-start
  0.7 1.2 %copy-done = bf16[1024,2,256]{2,1,0:T(2,128)(2,1)S(1)} copy-done((bf16[1024,2,256]{2,1,0:T(2,128)(2,1)S(1)}, bf16[1024,2,256]{2,1,0:T(2,128)(2,1)}, u32[]{:S(2)}) %copy-start) | copy-done | bytes 1048600
  1.9 0.0 copy-start.1
  1.9 0.0 copy-start.2
  1.9 0.0 copy-start.3
  1.9 0.0 copy-start.4
  1.9 0.0 copy-start.5
  1.9 0.0 copy-start.6
  1.9 0.0 copy-start.7
  1.9 9.8 %fusion.2 = bf16[4096,2,256]{2,0,1:T(8,128)(2,1)} fusion(bf16[1024,4096]{1,0:T(8,128)(2,1)} %param.9, bf16[1024,2,256]{2,1,0:T(2,128)(2,1)S(1)} %copy-done), kind=kOutput, calls=%fused_computation.2 | convolution fusion | flops 4297064448 | bytes 13631488 | tf_op jit(solution)/shard_map/tf,tjc->fjc/dot_general | solution.py:371
  11.8 0.0 copy-done.1
  11.8 0.0 copy-done.2
  11.8 0.0 copy-done.3
  11.8 0.0 copy-done.4
  11.8 0.0 copy-done.5
  11.8 0.0 copy-done.6
  11.8 0.0 copy-done.7
  11.8 79.7 %shard_map.152 = (f32[256,128]{1,0:T(8,128)S(1)}, f32[256,128]{1,0:T(8,128)S(1)}, f32[256,128]{1,0:T(8,128)S(1)}, bf16[4,2,8,256,128]{4,3,2,1,0:T(8,128)(2,1)S(1...) custom-call(bf16[2,4,2,8,64,256]{5,4,3,2,1,0:T(8,128)(2,1)} %bitcast, ...), custom_call_target="tpu_custom_call" | custom-call | tf_op jit(solution)/shard_map/pallas_call | solution.py:384
  91.5 2.3 %shard_map.153 = (f32[256,128]{1,0:T(8,128)}, f32[256,128]{1,0:T(8,128)}, f32[256,128]{1,0:T(8,128)}, bf16[4,2,8,256,128]{4,3,2,1,0:T(8,128)(2,1)}, f32[10,1024]...) custom-call(f32[256,128]{1,0:T(8,128)S(1)} %get-tuple-element.24.refs_0_, ...), custom_call_target="tpu_custom_call" | custom-call | tf_op jit(solution)/shard_map/pallas_call | solution.py:426
Async XLA Ops:
  0.6 1.2 %copy-start = (bf16[1024,2,256]{2,1,0:T(2,128)(2,1)S(1)}, bf16[1024,2,256]{2,1,0:T(2,128)(2,1)}, u32[]{:S(2)}) copy-start(bf16[1024,2,256]{2,1,0:T(2,128)(2,1)} %param.10) | copy-start | bytes 3145732
  1.9 9.9 %copy-start.1 = (f32[64,2,256]{2,1,0:T(2,128)S(1)}, f32[64,2,256]{2,1,0:T(2,128)}, u32[]{:S(2)}) copy-start(f32[64,2,256]{2,1,0:T(2,128)} %param.12) | copy-start | bytes 393220
  1.9 9.9 %copy-start.2 = (f32[64,2,256]{2,1,0:T(2,128)S(1)}, f32[64,2,256]{2,1,0:T(2,128)}, u32[]{:S(2)}) copy-start(f32[64,2,256]{2,1,0:T(2,128)} %param.13) | copy-start | bytes 393220
  1.9 9.9 %copy-start.3 = (f32[64,2,256]{2,1,0:T(2,128)S(1)}, f32[64,2,256]{2,1,0:T(2,128)}, u32[]{:S(2)}) copy-start(f32[64,2,256]{2,1,0:T(2,128)} %param.14) | copy-start | bytes 393220
  1.9 9.9 %copy-start.4 = (f32[10,1024]{1,0:T(8,128)S(1)}, f32[10,1024]{1,0:T(8,128)}, u32[]{:S(2)}) copy-start(f32[10,1024]{1,0:T(8,128)} %sm.1) | copy-start | bytes 122884
  1.9 9.9 %copy-start.5 = (f32[10,1024]{1,0:T(8,128)S(1)}, f32[10,1024]{1,0:T(8,128)}, u32[]{:S(2)}) copy-start(f32[10,1024]{1,0:T(8,128)} %s1_.1) | copy-start | bytes 122884
  1.9 9.9 %copy-start.6 = (f32[10,1024]{1,0:T(8,128)S(1)}, f32[10,1024]{1,0:T(8,128)}, u32[]{:S(2)}) copy-start(f32[10,1024]{1,0:T(8,128)} %s2_.1) | copy-start | bytes 122884
  1.9 9.9 %copy-start.7 = (bf16[1,10,1024]{2,1,0:T(8,128)(2,1)S(1)}, bf16[1,10,1024]{2,1,0:T(8,128)(2,1)}, u32[]{:S(2)}) copy-start(bf16[1,10,1024]{2,1,0:T(8,128)(2,1)} %param.11) | copy-start | bytes 61444

commit v3 on v2

v3 whole, which is shorter than its diff:
```python
import functools
import math

import jax
import jax.numpy as jnp
from jax import lax
from jax.experimental import pallas as pl
from jax.experimental.pallas import tpu as pltpu
from jax.sharding import PartitionSpec as P

D = 4096
EXPERTS = 8
STEP = 10
KV_COLS = 1024
SMALL_ROWS = 10

beta_one = 0.9
beta_two = 0.95
learning_rate = 0.01
weight_decay = 0.1
epsilon = 1e-08
clip_factor = 0.5

F32 = jnp.float32
BF16 = jnp.bfloat16
MESH = pl.DeviceIdType.MESH

ROWS = 64
HALF = 256
Z_FIRST = 32
LAST_Z = 96


def adamw(gradient, scale, first, second, master, decay):
    clipped = gradient * scale
    first_new = beta_one * first + (1.0 - beta_one) * clipped
    second_new = beta_two * second + (1.0 - beta_two) * clipped * clipped
    first_hat = first_new / (1.0 - beta_one**STEP)
    second_hat = second_new / (1.0 - beta_two**STEP)
    master_new = master - learning_rate * (
        first_hat / (jnp.sqrt(second_hat) + epsilon) + decay * master
    )
    return (master_new, first_new, second_new)


def folded(square):
    return square.reshape(-1, 8, 128).sum(axis=0)


def kernel(
    ny, nx, nz,
    inputs, *refs,
):
    held = refs[:8]
    om, o1, o2, gat, osm, os1, os2, osw = refs[8:16]
    cotangent, small, mw, m1, m2, sm, s1, s2 = refs[16:24]
    (
        xv, wide, flat, gs, own, pair, zc, zr, yc, yr, sy, syf, ry, sz, szf, rz, own_grad,
        smz, smr, smc, smy, smf, nzc, nyx,
        in_s, x_s, pair_s, pair_r, zc_s, zc_r, yc_s, yc_r, sy_s, sy_r, sz_s, sz_r,
        smz_s, smz_r, smc_s, smc_r, smy_s, smy_r, smf_s, smf_r,
        nzc_s, nzc_r, nyx_s, nyx_r,
        a1_s, a1_r, b1_s, b1_r, gc_s, gc_r, b2_s, b2_r, b3_s, b3_r, fa_s, fa_r, fb_s, fb_r,
    ) = refs[24:]
    shard = lax.axis_index("shard")
    x = lax.axis_index("tensor")
    z = lax.axis_index("section")
    y, c = shard // 2, shard % 2
    other = 1 - c
    sibling = (y * 2 + other, x, z)

    def at_y(d):
        yy = (y + d) % ny
        return yy, (yy * 2 + c, x, z)

    def at_z(d):
        zz = (z + d) % nz
        return zz, (shard, x, zz)

    def at_zc(d):
        zz, cc = (z + d // 2) % nz, (c + d % 2) % 2
        return zz * 2 + cc, (y * 2 + cc, x, zz)

    def at_yx(d):
        yy, xx = (y + d // nx) % ny, (x + d % nx) % nx
        return yy * nx + xx, (yy * 2 + c, xx, z)

    def copy(src, dst, send, recv, device):
        return pltpu.make_async_remote_copy(
            src_ref=src, dst_ref=dst, send_sem=send, recv_sem=recv, device_id=device, device_id_type=MESH
        )

    sent = []

    def send(*a):
        made = copy(*a)
        made.start()
        sent.append(made)

    fills = [pltpu.make_async_copy(held[i], refs[16 + i], in_s.at[i]) for i in range(8)]
    fills[0].start()

    order = (2, 1, 3, 0)
    loads = {}
    for i, d in enumerate(order):
        for half, core in enumerate((other, c)):
            start = pl.multiple_of((at_y(d)[0] * 2 + core) * (nz * ROWS), nz * ROWS)
            slot = 2 * i + half
            loads[d, half] = slot, pltpu.make_async_copy(
                inputs.at[:, pl.ds(start, nz * ROWS)], xv.at[slot], x_s.at[slot]
            )
            loads[d, half][1].start()

    for fill in fills[1:]:
        fill.start()

    barrier = pltpu.get_barrier_semaphore()
    peers = [at_zc(d)[1] for d in range(1, 2 * nz)] + [at_yx(d)[1] for d in range(1, ny * nx)]
    for peer in peers:
        pl.semaphore_signal(barrier, inc=1, device_id=peer, device_id_type=MESH)

    tokens = flat.shape[0]
    fills[0].wait()
    wide[...] = cotangent[...].astype(F32)
    for j in range(2):
        for q in range(2):
            flat[:, j * HALF + q * 128 : j * HALF + (q + 1) * 128] = wide[
                pl.ds(2 * q + j, tokens, stride=4), :
            ].astype(BF16)

    def summed(d, half):
        slot, load = loads[d, half]
        load.wait()
        made = lax.dot_general(
            xv[slot], flat[...], (((0,), (0,)), ((), ())), preferred_element_type=F32
        )
        return made.reshape(nz, ROWS, 2 * HALF)

    def swap(d):
        yy, _ = at_y(d)
        return copy(gs.at[yy], pair.at[yy], pair_s.at[d], pair_r.at[yy], sibling)

    def other_half(d):
        gs[at_y(d)[0]] = summed(d, 0).astype(BF16)

    def own_half(d):
        own[at_y(d)[0]] = summed(d, 1)

    def start_swap(d):
        made = swap(d)
        made.start()
        sent.append(made)

    def columns(j):
        return slice(j * HALF, (j + 1) * HALF)

    def own_z(j, zz):
        rows = slice(0, Z_FIRST)
        return own[:, zz, rows, columns(j)] + pair[:, zz, rows, columns(j)].astype(F32)

    def own_y(j, yy):
        rows = slice(Z_FIRST, ROWS)
        return own[yy, :, rows, columns(j)] + pair[yy, :, rows, columns(j)].astype(F32)

    z_hops = {(j, way): nz // 2 - (j ^ way) for j in range(2) for way in range(2)}
    y_hops = {(j, way): ny // 2 - (j ^ way) for j in range(2) for way in range(2)}

    def chain(own_part, at, size, at_me, hops, buffers, sems, j, way, k):
        sign = 1 if way == 0 else size - 1
        out, arrived = buffers
        if k:
            copy(out.at[j, way, k - 1], arrived.at[j, way, k - 1], sems[0].at[j, way, k - 1], sems[1].at[j, way, k - 1], at(sign)[1]).wait_recv()
        if k == hops[j, way]:
            return arrived[j, way, k - 1].astype(F32)
        total = own_part(j, (at_me + sign * (hops[j, way] - k)) % size)
        if k:
            total = total + arrived[j, way, k - 1].astype(F32)
        out[j, way, k] = total.astype(BF16)
        send(out.at[j, way, k], arrived.at[j, way, k], sems[0].at[j, way, k], sems[1].at[j, way, k], at(sign)[1])

    step_z = functools.partial(chain, own_z, at_z, nz, z, z_hops, (zc, zr), (zc_s, zc_r))
    step_y = functools.partial(chain, own_y, at_y, ny, y, y_hops, (yc, yr), (yc_s, yc_r))

    other_half(2)
    pl.semaphore_wait(barrier, len(peers))
    start_swap(2)

    fills[1].wait()
    smz[...] = jnp.zeros_like(smz)
    for i in range(nz):
        smz[i, 0:SMALL_ROWS, :] = small[:, i * 128 : (i + 1) * 128].astype(F32)
    smr[z] = smz[z]
    for d in range(1, nz):
        zz, peer = at_z(d)
        send(smz.at[zz], smr.at[z], smz_s.at[d], smz_r.at[z], peer)

    own_half(2)
    other_half(1)
    start_swap(1)
    swap(2).wait_recv()
    step_y(0, 0, 0)
    step_y(1, 1, 0)
    own_half(1)
    other_half(3)
    start_swap(3)
    swap(1).wait_recv()
    step_y(1, 0, 0)
    own_half(3)
    other_half(0)
    start_swap(0)
    swap(3).wait_recv()
    step_y(0, 1, 0)
    own_half(0)
    swap(0).wait_recv()
    for j, way in z_hops:
        step_z(j, way, 0)
    step_y(0, 0, 1)
    step_y(1, 1, 1)

    for d in range(1, nz):
        zz, peer = at_z(d)
        copy(smz.at[zz], smr.at[zz], smz_s.at[d], smz_r.at[zz], peer).wait_recv()
    block = smr[0]
    for i in range(1, nz):
        block = block + smr[i]
    smc[c] = block
    send(smc.at[c], smc.at[c], smc_s.at[0], smc_r.at[c], sibling)

    def steps_z(k):
        for j, way in z_hops:
            if k < z_hops[j, way]:
                step_z(j, way, k)

    steps_z(1)
    copy(smc.at[c], smc.at[other], smc_s.at[0], smc_r.at[other], sibling).wait_recv()
    smy[y] = smc[0] + smc[1]
    for d in range(1, ny):
        yy, peer = at_y(d)
        send(smy.at[y], smy.at[y], smy_s.at[d], smy_r.at[y], peer)
    steps_z(2)

    for j in range(2):
        total = own_y(j, y)
        for way in range(2):
            total = total + step_y(j, way, y_hops[j, way])
        szf[:, :, columns(j)] = total
        sz[:, :, columns(j)] = total.astype(BF16)
    for d in range(1, nz):
        zz, peer = at_z(d)
        send(sz.at[zz], rz.at[z], sz_s.at[d], sz_r.at[z], peer)
    for k in range(3, nz // 2):
        steps_z(k)
    for d in range(1, ny):
        yy, peer = at_y(d)
        copy(smy.at[y], smy.at[yy], smy_s.at[d], smy_r.at[yy], peer).wait_recv()
    block = smy[0]
    for i in range(1, ny):
        block = block + smy[i]
    smf[z] = block
    for d in range(1, nz):
        zz, peer = at_z(d)
        send(smf.at[z], smf.at[z], smf_s.at[d], smf_r.at[z], peer)

    for j in range(2):
        total = own_z(j, z)
        for way in range(2):
            total = total + step_z(j, way, z_hops[j, way])
        syf[:, :, columns(j)] = total
        sy[:, :, columns(j)] = total.astype(BF16)
    for d in range(1, ny):
        yy, peer = at_y(d)
        send(sy.at[yy], ry.at[y], sy_s.at[d], sy_r.at[y], peer)

    def place(total, start):
        for j in range(2):
            for q in range(2):
                at = j * HALF + q * 128
                own_grad[pl.ds(4 * start + 2 * q + j, total.shape[0], stride=4), :] = total[:, at : at + 128]

    for d in range(1, nz):
        zz, peer = at_z(d)
        copy(sz.at[zz], rz.at[zz], sz_s.at[d], sz_r.at[zz], peer).wait_recv()
    total = szf[z]
    for d in range(1, nz):
        total = total + rz[(z + d) % nz].astype(F32)
    place(total, Z_FIRST)
    for d in range(1, nz):
        zz, peer = at_z(d)
        copy(smf.at[z], smf.at[zz], smf_s.at[d], smf_r.at[zz], peer).wait_recv()
    small_square = jnp.zeros((8, 128), F32)
    for i in range(nz):
        rows = smf[i]
        small_square = small_square + folded(rows * rows)
    for d in range(1, ny):
        yy, peer = at_y(d)
        copy(sy.at[yy], ry.at[yy], sy_s.at[d], sy_r.at[yy], peer).wait_recv()
    total = syf[y]
    for d in range(1, ny):
        total = total + ry[(y + d) % ny].astype(F32)
    place(total, 0)

    for fill in fills[2:]:
        fill.wait()
    grad = own_grad[...]
    here = z * 2 + c
    nzc[here] = folded(grad * grad)
    for d in range(1, 2 * nz):
        there, peer = at_zc(d)
        send(nzc.at[here], nzc.at[here], nzc_s.at[d], nzc_r.at[here], peer)
    for d in range(1, 2 * nz):
        there, peer = at_zc(d)
        copy(nzc.at[here], nzc.at[there], nzc_s.at[d], nzc_r.at[there], peer).wait_recv()
    part = small_square * (1.0 / ny)
    for i in range(2 * nz):
        part = part + nzc[i]
    here = y * nx + x
    nyx[here] = part
    for d in range(1, ny * nx):
        there, peer = at_yx(d)
        send(nyx.at[here], nyx.at[here], nyx_s.at[d], nyx_r.at[here], peer)
    for d in range(1, ny * nx):
        there, peer = at_yx(d)
        copy(nyx.at[here], nyx.at[there], nyx_s.at[d], nyx_r.at[there], peer).wait_recv()
    part = nyx[0]
    for i in range(1, ny * nx):
        part = part + nyx[i]
    total = jnp.sum(part, keepdims=True)
    limit = clip_factor * math.sqrt(2 * D * KV_COLS + SMALL_ROWS * D)
    scale = jnp.minimum(1.0, limit / (jnp.sqrt(total) + 1e-06))

    master_new, first_new, second_new = adamw(grad, scale, m1[...], m2[...], mw[...], weight_decay)
    gat[y, c, z] = master_new.astype(BF16)

    def z_block(core, zz, half):
        return gat.at[:, core, zz, half * (LAST_Z // 2) : (half + 1) * (LAST_Z // 2)]

    def piece(core, yy, zz):
        return gat.at[yy, core, zz, LAST_Z:256]

    def half_piece(core, yy, zz, way):
        middle = (LAST_Z + 256) // 2
        return gat.at[yy, core, zz, slice(LAST_Z, middle) if way == 0 else slice(middle, 256)]

    def on_both_y(zz):
        for way in range(2):
            part = piece(c, y, zz)
            send(part, part, b2_s.at[way, zz], b2_r.at[way, zz], at_y(1 if way == 0 else ny - 1)[1])
        send(piece(c, y, zz), piece(c, y, zz), fb_s.at[0, zz], fb_r.at[0, zz], sibling)

    def relay_y(zz):
        for way in range(2):
            sign = 1 if way == 0 else ny - 1
            behind, source = at_y(ny - sign)
            part = piece(c, behind, zz)
            copy(part, part, b2_s.at[way, zz], b2_r.at[way, zz], source).wait_recv()
            half = half_piece(c, behind, zz, way)
            send(half, half, b3_s.at[way, zz], b3_r.at[way, zz], at_y(sign)[1])
            send(part, part, fb_s.at[1 + way, zz], fb_r.at[1 + way, zz], sibling)

    def far_y(zz):
        across, source = at_y(ny // 2)
        for way in range(2):
            half = half_piece(c, across, zz, way)
            copy(half, half, b3_s.at[way, zz], b3_r.at[way, zz], source).wait_recv()
        send(piece(c, across, zz), piece(c, across, zz), fb_s.at[3, zz], fb_r.at[3, zz], sibling)

    b_hops = (nz // 2, nz // 2 - 1)

    def step_b(way, k):
        sign = 1 if way == 0 else nz - 1
        zz = (z + (nz - sign) * k) % nz
        part = piece(c, y, zz)
        if k:
            copy(part, part, b1_s.at[way, k - 1], b1_r.at[way, k - 1], at_z(nz - sign)[1]).wait_recv()
        if k < b_hops[way]:
            send(part, part, b1_s.at[way, k], b1_r.at[way, k], at_z(sign)[1])
        if k or way == 0:
            on_both_y(zz)

    def step_g(half, way, k):
        sign = 1 if way == 0 else nz - 1
        zz = (z + (nz - sign) * k) % nz
        part = z_block(c, zz, half)
        if k:
            copy(part, part, gc_s.at[half, way, k - 1], gc_r.at[half, way, k - 1], at_z(nz - sign)[1]).wait_recv()
        if k < z_hops[half, way]:
            send(part, part, gc_s.at[half, way, k], gc_r.at[half, way, k], at_z(sign)[1])
        if k or way == 0:
            send(part, part, fa_s.at[half, way, k], fa_r.at[half, way, k], sibling)

    def around(k):
        return [(z + (nz - k if way == 0 else k)) % nz for way in range(2) if k <= b_hops[way] and (k or way == 0)]

    step_b(0, 0)
    step_b(1, 0)
    for d in range(1, ny):
        yy, peer = at_y(d)
        part = gat.at[y, c, z, 0:LAST_Z]
        send(part, part, a1_s.at[d], a1_r.at[y], peer)

    om[...] = master_new
    o1[...] = first_new
    o2[...] = second_new

    for d in range(1, ny):
        yy, peer = at_y(d)
        part = gat.at[yy, c, z, 0:LAST_Z]
        copy(part, part, a1_s.at[d], a1_r.at[yy], peer).wait_recv()
    for half, way in z_hops:
        step_g(half, way, 0)
    for zz in around(0):
        relay_y(zz)

    decay = jnp.where(lax.broadcasted_iota(jnp.int32, (SMALL_ROWS, 128), 0) < EXPERTS, weight_decay, 0.0).astype(F32)
    for k in range(1, nz // 2 + 1):
        for way in range(2):
            if k <= b_hops[way]:
                step_b(way, k)
        for half, way in z_hops:
            if k <= z_hops[half, way]:
                step_g(half, way, k)
        for zz in around(k - 1):
            far_y(zz)
        for zz in around(k):
            relay_y(zz)
        if k == 1:
            for i in range(nz):
                lanes = slice(i * 128, (i + 1) * 128)
                made = adamw(smf[i, 0:SMALL_ROWS, :], scale, s1[:, lanes], s2[:, lanes], sm[:, lanes], decay)
                osm[:, lanes], os1[:, lanes], os2[:, lanes] = made
                osw[:, lanes] = made[0].astype(BF16)
    for zz in around(nz // 2):
        far_y(zz)

    for half, way in z_hops:
        for k in range(way, z_hops[half, way] + 1):
            zz = (z + (nz - k if way == 0 else k)) % nz
            copy(z_block(c, zz, half), z_block(other, zz, half), fa_s.at[half, way, k], fa_r.at[half, way, k], sibling).wait_recv()
    for i, d in enumerate((0, ny - 1, 1, ny // 2)):
        yy, _ = at_y(d)
        for zz in range(nz):
            copy(piece(c, yy, zz), piece(other, yy, zz), fb_s.at[i, zz], fb_r.at[i, zz], sibling).wait_recv()
    for made in sent:
        made.wait_send()


def leave(count, *refs):
    semaphores = refs[2 * count]
    copies = [pltpu.make_async_copy(refs[i], refs[count + i], semaphores.at[i]) for i in range(count)]
    for made in copies:
        made.start()
    for made in copies:
        made.wait()


def stored(array):
    rows = array.shape[0]
    return array.reshape(rows, 2, 2, 128).transpose(0, 2, 1, 3).reshape(rows * 4, 128)


def unstored(array):
    rows = array.shape[0] // 4
    return array.reshape(rows, 2, 2, 128).transpose(0, 2, 1, 3).reshape(rows, 2, 256)


def body(
    ny, nx, nz,
    normed_inputs,
    projection_cotangent,
    small_partials,
    master_weights,
    first_moment,
    second_moment,
    small_master,
    small_first,
    small_second,
):
    tokens, features = normed_inputs.shape
    assert ny == 4 and features == ny * 2 * nz * ROWS
    small_shape = jax.ShapeDtypeStruct(small_master.shape, F32)
    owned = jax.ShapeDtypeStruct((4 * ROWS, 128), F32)
    dma = pltpu.SemaphoreType.DMA
    vm = pltpu.VMEM
    last = ROWS - Z_FIRST
    along_y, along_z = [dma((ny,))] * 2, [dma((nz,))] * 2
    pairs, chains = [dma((2,))] * 2, [dma((2, 2, nz // 2))] * 2
    given = (
        normed_inputs, stored(projection_cotangent), small_partials[0],
        stored(master_weights), stored(first_moment), stored(second_moment),
        small_master, small_first, small_second,
    )
    given = [pltpu.with_memory_space_constraint(array, pltpu.HBM) for array in given]
    outs = pl.pallas_call(
        functools.partial(kernel, ny, nx, nz),
        out_shape=(
            owned, owned, owned,
            jax.ShapeDtypeStruct((ny, 2, nz, 4 * ROWS, 128), BF16),
            small_shape, small_shape, small_shape,
            jax.ShapeDtypeStruct(small_master.shape, BF16),
        ),
        in_specs=[pl.BlockSpec(memory_space=pltpu.HBM)] * 9,
        out_specs=[pl.BlockSpec(memory_space=pltpu.VMEM)] * 8,
        scratch_shapes=[
            *[vm(array.shape, array.dtype) for array in given[1:]],
            vm((2 * ny, tokens, nz * ROWS), BF16),
            vm((4 * tokens, 128), F32),
            vm((tokens, 2 * HALF), BF16),
            vm((ny, nz, ROWS, 2 * HALF), BF16),
            vm((ny, nz, ROWS, 2 * HALF), F32),
            vm((ny, nz, ROWS, 2 * HALF), BF16),
            *[vm((2, 2, nz // 2, ny, Z_FIRST, HALF), BF16)] * 2,
            *[vm((2, 2, ny // 2, nz, last, HALF), BF16)] * 2,
            vm((ny, Z_FIRST, 2 * HALF), BF16),
            vm((ny, Z_FIRST, 2 * HALF), F32),
            vm((ny, Z_FIRST, 2 * HALF), BF16),
            vm((nz, last, 2 * HALF), BF16),
            vm((nz, last, 2 * HALF), F32),
            vm((nz, last, 2 * HALF), BF16),
            vm((4 * ROWS, 128), F32),
            vm((nz, 16, 128), F32),
            vm((nz, 16, 128), F32),
            vm((2, 16, 128), F32),
            vm((ny, 16, 128), F32),
            vm((nz, 16, 128), F32),
            vm((2 * nz, 8, 128), F32),
            vm((ny * nx, 8, 128), F32),
            dma((8,)), dma((2 * ny,)), *along_y, *chains, *[dma((2, 2, ny // 2))] * 2, *along_y, *along_z,
            *along_z, *pairs, *along_y, *along_z,
            *[dma((2 * nz,))] * 2, *[dma((ny * nx,))] * 2,
            *along_y, *[dma((2, nz // 2))] * 2, *chains, *[dma((2, nz))] * 4, *[dma((2, 2, nz // 2 + 1))] * 2, *[dma((4, nz))] * 2,
        ],
        compiler_params=pltpu.CompilerParams(
            collective_id=0, has_side_effects=True, vmem_limit_bytes=36 << 20
        ),
    )(*given)
    count = len(outs)
    outs = pl.pallas_call(
        functools.partial(leave, count),
        out_shape=[jax.ShapeDtypeStruct(o.shape, o.dtype) for o in outs],
        in_specs=[pl.BlockSpec(memory_space=pltpu.VMEM)] * count,
        out_specs=[pl.BlockSpec(memory_space=pl.ANY)] * count,
        scratch_shapes=[dma((count,))],
        compiler_params=pltpu.CompilerParams(vmem_limit_bytes=16 << 20),
    )(*outs)
    return (
        unstored(outs[0]), unstored(outs[1]), unstored(outs[2]),
        unstored(outs[3].reshape(-1, 128)),
        outs[4], outs[5], outs[6], outs[7],
    )


def solution(mesh):
    ny, nx, nz = mesh.shape["shard"] // 2, mesh.shape["tensor"], mesh.shape["section"]
    rows = P(("shard", "section"), None, "tensor")
    flat = P(None, "tensor")
    return jax.shard_map(
        functools.partial(body, ny, nx, nz),
        mesh=mesh,
        in_specs=(P(("shard", "section"), None), rows, rows, rows, rows, rows, flat, flat, flat),
        out_specs=(rows, rows, rows, P(None, None, "tensor"), flat, flat, flat, flat),
        check_vma=False,
    )
```

time: 93.9 us -> 86.1 us (0.917)
  matrix products: 9.85 us -> 0 us
  Pallas kernels: 81.9 us -> 85.3 us
  local copies, waits for them, and re-layouts: 1.25 us -> 0 us
    dot_general x1 -> x0, matrix products: 9.85 us -> none  [body(): jnp.einsum('tf,tjc->fjc', normed_inputs, projection_cotangent, preferred_...]
    pallas_call x1, Pallas kernels: 79.7 us -> 83.1 us  [body(): pl.pallas_call(functools.partial(kernel, ny, nx, nz), out_shape=(owned, o...]
    unnamed x16 -> x0, local copies, waits for them, and re-layouts: 1.25 us -> none
where the time goes in v3:
time: 86.1 us; the launch traced here: 86 us
  Pallas kernels  85.3 us (99%)
    pallas_call x1, Pallas kernels, body(): pl.pallas_call(functools.partial(kernel, ny, nx, nz), out_shape=(owned, o...  83.1 us
    pallas_call x1, Pallas kernels, body(): pl.pallas_call(functools.partial(leave, count), out_shape=[jax.ShapeDtype...  2.26 us

profile of v3, /device:TPU:1, one launch (start us, length us, event | category | flops | bytes accessed | tf_op | source)
XLA Modules:
  0.0 86.0 jit_solution(8968396115776587096)
XLA Ops:
  0.6 83.1 %shard_map.152 = (f32[256,128]{1,0:T(8,128)S(1)}, f32[256,128]{1,0:T(8,128)S(1)}, f32[256,128]{1,0:T(8,128)S(1)}, bf16[4,2,8,256,128]{4,3,2,1,0:T(8,128)(2,1)S(1...) custom-call(bf16[1024,4096]{1,0:T(8,128)(2,1)} %inputs.1, ...), custom_call_target="tpu_custom_call" | custom-call | tf_op jit(solution)/shard_map/pallas_call | solution.py:493
  83.7 2.3 %shard_map.153 = (f32[256,128]{1,0:T(8,128)}, f32[256,128]{1,0:T(8,128)}, f32[256,128]{1,0:T(8,128)}, bf16[4,2,8,256,128]{4,3,2,1,0:T(8,128)(2,1)}, f32[10,1024]...) custom-call(f32[256,128]{1,0:T(8,128)S(1)} %get-tuple-element.24.refs_0_, ...), custom_call_target="tpu_custom_call" | custom-call | tf_op jit(solution)/shard_map/pallas_call | solution.py:537

commit v4 on v3

--- a/solution.py
+++ b/solution.py
@@ -28,7 +28,7 @@
 ROWS = 64
 HALF = 256
 Z_FIRST = 32
-LAST_Z = 96
+LAST_Z = 64
 
 
 def adamw(gradient, scale, first, second, master, decay):
@@ -55,9 +55,9 @@
     om, o1, o2, gat, osm, os1, os2, osw = refs[8:16]
     cotangent, small, mw, m1, m2, sm, s1, s2 = refs[16:24]
     (
-        xv, wide, flat, gs, own, pair, zc, zr, yc, yr, sy, syf, ry, sz, szf, rz, own_grad,
+        xv, wide, flat, gs, own, pair, zc, zr, yc, yr, sy, syf, ry, wc, wr, szf, own_grad,
         smz, smr, smc, smy, smf, nzc, nyx,
-        in_s, x_s, pair_s, pair_r, zc_s, zc_r, yc_s, yc_r, sy_s, sy_r, sz_s, sz_r,
+        in_s, x_s, pair_s, pair_r, zc_s, zc_r, yc_s, yc_r, sy_s, sy_r, wc_s, wc_r,
         smz_s, smz_r, smc_s, smc_r, smy_s, smy_r, smf_s, smf_r,
         nzc_s, nzc_r, nyx_s, nyx_r,
         a1_s, a1_r, b1_s, b1_r, gc_s, gc_r, b2_s, b2_r, b3_s, b3_r, fa_s, fa_r, fb_s, fb_r,
@@ -161,6 +161,9 @@
     def own_y(j, yy):
         rows = slice(Z_FIRST, ROWS)
         return own[yy, :, rows, columns(j)] + pair[yy, :, rows, columns(j)].astype(F32)
+
+    def own_w(j, zz):
+        return szf[zz, :, columns(j)]
 
     z_hops = {(j, way): nz // 2 - (j ^ way) for j in range(2) for way in range(2)}
     y_hops = {(j, way): ny // 2 - (j ^ way) for j in range(2) for way in range(2)}
@@ -179,6 +182,7 @@
         send(out.at[j, way, k], arrived.at[j, way, k], sems[0].at[j, way, k], sems[1].at[j, way, k], at(sign)[1])
 
     step_z = functools.partial(chain, own_z, at_z, nz, z, z_hops, (zc, zr), (zc_s, zc_r))
+    step_w = functools.partial(chain, own_w, at_z, nz, z, z_hops, (wc, wr), (wc_s, wc_r))
     step_y = functools.partial(chain, own_y, at_y, ny, y, y_hops, (yc, yr), (yc_s, yc_r))
 
     other_half(2)
@@ -226,30 +230,28 @@
     smc[c] = block
     send(smc.at[c], smc.at[c], smc_s.at[0], smc_r.at[c], sibling)
 
-    def steps_z(k):
+    def steps(step, k):
         for j, way in z_hops:
             if k < z_hops[j, way]:
-                step_z(j, way, k)
-
-    steps_z(1)
+                step(j, way, k)
+
+    steps(step_z, 1)
     copy(smc.at[c], smc.at[other], smc_s.at[0], smc_r.at[other], sibling).wait_recv()
     smy[y] = smc[0] + smc[1]
     for d in range(1, ny):
         yy, peer = at_y(d)
         send(smy.at[y], smy.at[y], smy_s.at[d], smy_r.at[y], peer)
-    steps_z(2)
 
     for j in range(2):
         total = own_y(j, y)
         for way in range(2):
             total = total + step_y(j, way, y_hops[j, way])
         szf[:, :, columns(j)] = total
-        sz[:, :, columns(j)] = total.astype(BF16)
-    for d in range(1, nz):
-        zz, peer = at_z(d)
-        send(sz.at[zz], rz.at[z], sz_s.at[d], sz_r.at[z], peer)
+    steps(step_w, 0)
+    steps(step_z, 2)
+    steps(step_w, 1)
     for k in range(3, nz // 2):
-        steps_z(k)
+        steps(step_z, k)
     for d in range(1, ny):
         yy, peer = at_y(d)
         copy(smy.at[y], smy.at[yy], smy_s.at[d], smy_r.at[yy], peer).wait_recv()
@@ -260,6 +262,7 @@
     for d in range(1, nz):
         zz, peer = at_z(d)
         send(smf.at[z], smf.at[z], smf_s.at[d], smf_r.at[z], peer)
+    steps(step_w, 2)
 
     for j in range(2):
         total = own_z(j, z)
@@ -270,20 +273,13 @@
     for d in range(1, ny):
         yy, peer = at_y(d)
         send(sy.at[yy], ry.at[y], sy_s.at[d], sy_r.at[y], peer)
-
-    def place(total, start):
-        for j in range(2):
-            for q in range(2):
-                at = j * HALF + q * 128
-                own_grad[pl.ds(4 * start + 2 * q + j, total.shape[0], stride=4), :] = total[:, at : at + 128]
-
-    for d in range(1, nz):
-        zz, peer = at_z(d)
-        copy(sz.at[zz], rz.at[zz], sz_s.at[d], sz_r.at[zz], peer).wait_recv()
-    total = szf[z]
-    for d in range(1, nz):
-        total = total + rz[(z + d) % nz].astype(F32)
-    place(total, Z_FIRST)
+    for k in range(3, nz // 2):
+        steps(step_w, k)
+
+    def place(total, start, j):
+        for q in range(2):
+            own_grad[pl.ds(4 * start + 2 * q + j, total.shape[0], stride=4), :] = total[:, q * 128 : (q + 1) * 128]
+
     for d in range(1, nz):
         zz, peer = at_z(d)
         copy(smf.at[z], smf.at[zz], smf_s.at[d], smf_r.at[zz], peer).wait_recv()
@@ -294,10 +290,16 @@
     for d in range(1, ny):
         yy, peer = at_y(d)
         copy(sy.at[yy], ry.at[yy], sy_s.at[d], sy_r.at[yy], peer).wait_recv()
-    total = syf[y]
-    for d in range(1, ny):
-        total = total + ry[(y + d) % ny].astype(F32)
-    place(total, 0)
+    for j in range(2):
+        total = syf[y, :, columns(j)]
+        for d in range(1, ny):
+            total = total + ry[(y + d) % ny, :, columns(j)].astype(F32)
+        place(total, 0, j)
+    for j in range(2):
+        total = own_w(j, z)
+        for way in range(2):
+            total = total + step_w(j, way, z_hops[j, way])
+        place(total, Z_FIRST, j)
 
     for fill in fills[2:]:
         fill.wait()
@@ -408,9 +410,6 @@
         copy(part, part, a1_s.at[d], a1_r.at[yy], peer).wait_recv()
     for half, way in z_hops:
         step_g(half, way, 0)
-    for zz in around(0):
-        relay_y(zz)
-
     decay = jnp.where(lax.broadcasted_iota(jnp.int32, (SMALL_ROWS, 128), 0) < EXPERTS, weight_decay, 0.0).astype(F32)
     for k in range(1, nz // 2 + 1):
         for way in range(2):
@@ -420,9 +419,9 @@
             if k <= z_hops[half, way]:
                 step_g(half, way, k)
         for zz in around(k - 1):
+            relay_y(zz)
+        for zz in around(k - 2) if k > 1 else ():
             far_y(zz)
-        for zz in around(k):
-            relay_y(zz)
         if k == 1:
             for i in range(nz):
                 lanes = slice(i * 128, (i + 1) * 128)
@@ -430,7 +429,10 @@
                 osm[:, lanes], os1[:, lanes], os2[:, lanes] = made
                 osw[:, lanes] = made[0].astype(BF16)
     for zz in around(nz // 2):
-        far_y(zz)
+        relay_y(zz)
+    for k in (nz // 2 - 1, nz // 2):
+        for zz in around(k):
+            far_y(zz)
 
     for half, way in z_hops:
         for k in range(way, z_hops[half, way] + 1):
@@ -513,9 +515,8 @@
             vm((ny, Z_FIRST, 2 * HALF), BF16),
             vm((ny, Z_FIRST, 2 * HALF), F32),
             vm((ny, Z_FIRST, 2 * HALF), BF16),
-            vm((nz, last, 2 * HALF), BF16),
+            *[vm((2, 2, nz // 2, last, HALF), BF16)] * 2,
             vm((nz, last, 2 * HALF), F32),
-            vm((nz, last, 2 * HALF), BF16),
             vm((4 * ROWS, 128), F32),
             vm((nz, 16, 128), F32),
             vm((nz, 16, 128), F32),
@@ -524,7 +525,7 @@
             vm((nz, 16, 128), F32),
             vm((2 * nz, 8, 128), F32),
             vm((ny * nx, 8, 128), F32),
-            dma((8,)), dma((2 * ny,)), *along_y, *chains, *[dma((2, 2, ny // 2))] * 2, *along_y, *along_z,
+            dma((8,)), dma((2 * ny,)), *along_y, *chains, *[dma((2, 2, ny // 2))] * 2, *along_y, *chains,
             *along_z, *pairs, *along_y, *along_z,
             *[dma((2 * nz,))] * 2, *[dma((ny * nx,))] * 2,
             *along_y, *[dma((2, nz // 2))] * 2, *chains, *[dma((2, nz))] * 4, *[dma((2, 2, nz // 2 + 1))] * 2, *[dma((4, nz))] * 2,

time: 86.1 us -> 80 us (0.929)
  Pallas kernels: 85.3 us -> 79.3 us
    pallas_call x1, Pallas kernels: 83.1 us -> 77 us  [body(): pl.pallas_call(functools.partial(kernel, ny, nx, nz), out_shape=(owned, o...]
where the time goes in v4:
time: 80 us; the launch traced here: 79.9 us
  Pallas kernels  79.3 us (99%)
    pallas_call x1, Pallas kernels, body(): pl.pallas_call(functools.partial(kernel, ny, nx, nz), out_shape=(owned, o...  77 us
    pallas_call x1, Pallas kernels, body(): pl.pallas_call(functools.partial(leave, count), out_shape=[jax.ShapeDtype...  2.26 us

profile of v4, /device:TPU:1, one launch (start us, length us, event | category | flops | bytes accessed | tf_op | source)
XLA Modules:
  0.0 79.9 jit_solution(5528145012883186074)
XLA Ops:
  0.6 77.0 %shard_map.152 = (f32[256,128]{1,0:T(8,128)S(1)}, f32[256,128]{1,0:T(8,128)S(1)}, f32[256,128]{1,0:T(8,128)S(1)}, bf16[4,2,8,256,128]{4,3,2,1,0:T(8,128)(2,1)S(1...) custom-call(bf16[1024,4096]{1,0:T(8,128)(2,1)} %inputs.1, ...), custom_call_target="tpu_custom_call" | custom-call | tf_op jit(solution)/shard_map/pallas_call | solution.py:495
  77.7 2.3 %shard_map.153 = (f32[256,128]{1,0:T(8,128)}, f32[256,128]{1,0:T(8,128)}, f32[256,128]{1,0:T(8,128)}, bf16[4,2,8,256,128]{4,3,2,1,0:T(8,128)(2,1)}, f32[10,1024]...) custom-call(f32[256,128]{1,0:T(8,128)S(1)} %get-tuple-element.24.refs_0_, ...), custom_call_target="tpu_custom_call" | custom-call | tf_op jit(solution)/shard_map/pallas_call | solution.py:538

commit v5 on v4

--- a/solution.py
+++ b/solution.py
@@ -28,7 +28,7 @@
 ROWS = 64
 HALF = 256
 Z_FIRST = 32
-LAST_Z = 64
+LAST_Z = 32
 
 
 def adamw(gradient, scale, first, second, master, decay):
@@ -109,7 +109,8 @@
             loads[d, half] = slot, pltpu.make_async_copy(
                 inputs.at[:, pl.ds(start, nz * ROWS)], xv.at[slot], x_s.at[slot]
             )
-            loads[d, half][1].start()
+            if slot < 3:
+                loads[d, half][1].start()
 
     for fill in fills[1:]:
         fill.start()
@@ -131,6 +132,9 @@
     def summed(d, half):
         slot, load = loads[d, half]
         load.wait()
+        for later, following in loads.values():
+            if later == slot + 3:
+                following.start()
         made = lax.dot_general(
             xv[slot], flat[...], (((0,), (0,)), ((), ())), preferred_element_type=F32
         )
@@ -306,7 +310,7 @@
     grad = own_grad[...]
     here = z * 2 + c
     nzc[here] = folded(grad * grad)
-    for d in range(1, 2 * nz):
+    for d in sorted(range(1, 2 * nz), key=lambda d: -min(d // 2, nz - d // 2)):
         there, peer = at_zc(d)
         send(nzc.at[here], nzc.at[here], nzc_s.at[d], nzc_r.at[here], peer)
     for d in range(1, 2 * nz):
@@ -317,7 +321,7 @@
         part = part + nzc[i]
     here = y * nx + x
     nyx[here] = part
-    for d in range(1, ny * nx):
+    for d in sorted(range(1, ny * nx), key=lambda d: -min(d // nx, ny - d // nx) - min(d % nx, nx - d % nx)):
         there, peer = at_yx(d)
         send(nyx.at[here], nyx.at[here], nyx_s.at[d], nyx_r.at[here], peer)
     for d in range(1, ny * nx):
@@ -415,11 +419,11 @@
         for way in range(2):
             if k <= b_hops[way]:
                 step_b(way, k)
+        for zz in around(k - 1):
+            relay_y(zz)
         for half, way in z_hops:
             if k <= z_hops[half, way]:
                 step_g(half, way, k)
-        for zz in around(k - 1):
-            relay_y(zz)
         for zz in around(k - 2) if k > 1 else ():
             far_y(zz)
         if k == 1:

time: 80 us -> 79 us (0.988)
  Pallas kernels: 79.3 us -> 78.2 us
    pallas_call x1, Pallas kernels: 77 us -> 76 us  [body(): pl.pallas_call(functools.partial(kernel, ny, nx, nz), out_shape=(owned, o...]
where the time goes in v5:
time: 79 us; the launch traced here: 78.9 us
  Pallas kernels  78.2 us (99%)
    pallas_call x1, Pallas kernels, body(): pl.pallas_call(functools.partial(kernel, ny, nx, nz), out_shape=(owned, o...  76 us
    pallas_call x1, Pallas kernels, body(): pl.pallas_call(functools.partial(leave, count), out_shape=[jax.ShapeDtype...  2.26 us

profile of v5, /device:TPU:1, one launch (start us, length us, event | category | flops | bytes accessed | tf_op | source)
XLA Modules:
  0.0 78.9 jit_solution(17709299979057519770)
XLA Ops:
  0.6 76.0 %shard_map.152 = (f32[256,128]{1,0:T(8,128)S(1)}, f32[256,128]{1,0:T(8,128)S(1)}, f32[256,128]{1,0:T(8,128)S(1)}, bf16[4,2,8,256,128]{4,3,2,1,0:T(8,128)(2,1)S(1...) custom-call(bf16[1024,4096]{1,0:T(8,128)(2,1)} %inputs.1, ...), custom_call_target="tpu_custom_call" | custom-call | tf_op jit(solution)/shard_map/pallas_call | solution.py:499
  76.6 2.3 %shard_map.153 = (f32[256,128]{1,0:T(8,128)}, f32[256,128]{1,0:T(8,128)}, f32[256,128]{1,0:T(8,128)}, bf16[4,2,8,256,128]{4,3,2,1,0:T(8,128)(2,1)}, f32[10,1024]...) custom-call(f32[256,128]{1,0:T(8,128)S(1)} %get-tuple-element.24.refs_0_, ...), custom_call_target="tpu_custom_call" | custom-call | tf_op jit(solution)/shard_map/pallas_call | solution.py:542

commit v6 on v5

--- a/solution.py
+++ b/solution.py
@@ -378,7 +378,7 @@
         part = piece(c, y, zz)
         if k:
             copy(part, part, b1_s.at[way, k - 1], b1_r.at[way, k - 1], at_z(nz - sign)[1]).wait_recv()
-        if k < b_hops[way]:
+        if k < nz // 2 - 1:
             send(part, part, b1_s.at[way, k], b1_r.at[way, k], at_z(sign)[1])
         if k or way == 0:
             on_both_y(zz)
@@ -399,6 +399,8 @@
 
     step_b(0, 0)
     step_b(1, 0)
+    part = piece(c, y, z)
+    send(part, part, b1_s.at[0, nz // 2 - 1], b1_r.at[0, nz // 2 - 1], at_z(nz // 2)[1])
     for d in range(1, ny):
         yy, peer = at_y(d)
         part = gat.at[y, c, z, 0:LAST_Z]
@@ -415,16 +417,17 @@
     for half, way in z_hops:
         step_g(half, way, 0)
     decay = jnp.where(lax.broadcasted_iota(jnp.int32, (SMALL_ROWS, 128), 0) < EXPERTS, weight_decay, 0.0).astype(F32)
+    turns = [0, 1, nz // 2, *range(2, nz // 2)]
     for k in range(1, nz // 2 + 1):
         for way in range(2):
-            if k <= b_hops[way]:
-                step_b(way, k)
-        for zz in around(k - 1):
+            if turns[k] <= b_hops[way]:
+                step_b(way, turns[k])
+        for zz in around(turns[k - 1]):
             relay_y(zz)
         for half, way in z_hops:
             if k <= z_hops[half, way]:
                 step_g(half, way, k)
-        for zz in around(k - 2) if k > 1 else ():
+        for zz in around(turns[k - 2]) if k > 1 else ():
             far_y(zz)
         if k == 1:
             for i in range(nz):
@@ -432,9 +435,9 @@
                 made = adamw(smf[i, 0:SMALL_ROWS, :], scale, s1[:, lanes], s2[:, lanes], sm[:, lanes], decay)
                 osm[:, lanes], os1[:, lanes], os2[:, lanes] = made
                 osw[:, lanes] = made[0].astype(BF16)
-    for zz in around(nz // 2):
+    for zz in around(turns[-1]):
         relay_y(zz)
-    for k in (nz // 2 - 1, nz // 2):
+    for k in turns[-2:]:
         for zz in around(k):
             far_y(zz)
 

time: 79 us -> 80.1 us (1.014)
  Pallas kernels: 78.2 us -> 79.3 us
    pallas_call x1, Pallas kernels: 76 us -> 77.1 us  [body(): pl.pallas_call(functools.partial(kernel, ny, nx, nz), out_shape=(owned, o...]
where the time goes in v6:
time: 80.1 us; the launch traced here: 80 us
  Pallas kernels  79.3 us (99%)
    pallas_call x1, Pallas kernels, body(): pl.pallas_call(functools.partial(kernel, ny, nx, nz), out_shape=(owned, o...  77.1 us
    pallas_call x1, Pallas kernels, body(): pl.pallas_call(functools.partial(leave, count), out_shape=[jax.ShapeDtype...  2.26 us

profile of v6, /device:TPU:1, one launch (start us, length us, event | category | flops | bytes accessed | tf_op | source)
XLA Modules:
  0.0 80.0 jit_solution(1470590311275765589)
XLA Ops:
  0.6 77.1 %shard_map.152 = (f32[256,128]{1,0:T(8,128)S(1)}, f32[256,128]{1,0:T(8,128)S(1)}, f32[256,128]{1,0:T(8,128)S(1)}, bf16[4,2,8,256,128]{4,3,2,1,0:T(8,128)(2,1)S(1...) custom-call(bf16[1024,4096]{1,0:T(8,128)(2,1)} %inputs.1, ...), custom_call_target="tpu_custom_call" | custom-call | tf_op jit(solution)/shard_map/pallas_call | solution.py:502
  77.7 2.3 %shard_map.153 = (f32[256,128]{1,0:T(8,128)}, f32[256,128]{1,0:T(8,128)}, f32[256,128]{1,0:T(8,128)}, bf16[4,2,8,256,128]{4,3,2,1,0:T(8,128)(2,1)}, f32[10,1024]...) custom-call(f32[256,128]{1,0:T(8,128)S(1)} %get-tuple-element.24.refs_0_, ...), custom_call_target="tpu_custom_call" | custom-call | tf_op jit(solution)/shard_map/pallas_call | solution.py:545
